TPU v7x, 256 devices: a whole 4x4x8 slice. The times are simulated.
256 devices in a mesh: seq: 16 (over y_lo, z), chan: 16 (over y_hi, x, core).
Axes of the slice: x: 4, y: 4 (y_hi: 2, y_lo: 2; y = y_hi * 2 + y_lo), z: 8, core: 2. Of those that a mesh axis runs over, the one named last changes fastest.
Arguments:
- tokens: bfloat16 [8192, 8192], P('seq', 'chan'), may hold values from -6 to 6
- norm_gain: float32 [8192], replicated, may hold values from 0.1 to 1.9
- w_in: bfloat16 [8192, 3, 4096], P('seq', None, 'chan'), may hold values from -0.0625 to 0.0625
- short_taps: float32 [3, 3, 4096], P(None, None, 'chan'), may hold values from -3.6 to 3.6
- medium_taps: float32 [128, 256], P(None, 'chan'), may hold values from -0.75 to 0.75
- skip_gain: float32 [4096], P('chan'), may hold values from 0.5 to 1.5
- w_out: bfloat16 [4096, 8192], P('chan'), may hold values from -0.09375 to 0.09375
Outputs:
- block_out: bfloat16 [8192, 8192], P('seq', 'chan')
All inputs are finite; a program needn't handle non-finite values.
Results may differ from a plain program's by a relative error of at most 0.019.
Values may be sent and summed in bfloat16 or wider, within the bound.
A program may use at most 128 MiB of HBM per device.

v0:
```python
import jax
import jax.numpy as jnp
from jax import lax
from jax.sharding import PartitionSpec as P

TAPS = 128
GROUP = 16


EPSILON = 1e-06


def passed_along(value, axis, steps):
    count = lax.axis_size(axis)
    first, last = (max(0, -steps), min(count, count - steps))
    return lax.ppermute(value, axis, [(source, source + steps) for source in range(first, last)])


def short_filter(extended, taps):
    return taps[0] * extended[2:] + taps[1] * extended[1:-1] + taps[2] * extended[:-2]


def per_device(tokens, norm_gain, w_in, short_taps, medium_taps, skip_gain, w_out):
    row_count = tokens.shape[0]
    channels = w_in.shape[2]
    gathered = lax.all_gather(tokens, "chan", axis=1, tiled=True)
    widened = gathered.astype(jnp.float32)
    mean_square = jnp.mean(widened * widened, axis=1, keepdims=True)
    normed = (widened * lax.rsqrt(mean_square + EPSILON) * norm_gain).astype(jnp.bfloat16)
    section = lax.all_gather(w_in, "seq", axis=0, tiled=True)
    flat_section = section.reshape(section.shape[0], 3 * channels)
    summed = jnp.dot(normed, flat_section, preferred_element_type=jnp.float32)
    projected = summed.astype(jnp.bfloat16).reshape(row_count, 3, channels)
    edge_rows = passed_along(projected[row_count - 2 :], "seq", 1)
    extended = lax.optimization_barrier(jnp.concatenate([edge_rows, projected], 0)).astype(
        jnp.float32
    )
    filtered = short_filter(extended, short_taps)
    queries = filtered[:, 0]
    product = (filtered[:, 1] * filtered[:, 2]).astype(jnp.bfloat16)
    product_rows = passed_along(product[row_count - (TAPS - 1) :], "seq", 1)
    reached = jnp.concatenate([product_rows, product], 0)
    floats = lax.optimization_barrier(reached).astype(jnp.float32)
    padded = jnp.concatenate([jnp.zeros((1, channels), jnp.float32), floats], 0)
    block_count = row_count // TAPS
    blocks = padded.reshape(block_count + 1, TAPS, channels)
    windows = jnp.concatenate([blocks[:-1], blocks[1:]], 1)
    cube_shape = (TAPS, TAPS, 2 * TAPS)
    lagged = (
        lax.broadcasted_iota(jnp.int32, cube_shape, 1)
        + TAPS
        - lax.broadcasted_iota(jnp.int32, cube_shape, 2)
    )
    onehot = (lagged == lax.broadcasted_iota(jnp.int32, cube_shape, 0)).astype(jnp.float32)
    toeplitz = jnp.einsum("jg,jis->gis", medium_taps, onehot, precision=lax.Precision.HIGHEST)
    filters = medium_taps.shape[1]
    grouped = windows.reshape(block_count, 2 * TAPS, filters, GROUP)
    convolved = jnp.einsum("gis,bsgc->bigc", toeplitz, grouped, precision=lax.Precision.HIGHEST)
    mixing = skip_gain * floats[TAPS - 1 :] + convolved.reshape(row_count, channels)
    gating = (queries * mixing).astype(jnp.bfloat16)
    partial_out = jnp.dot(gating, w_out, preferred_element_type=jnp.float32)
    rounded_out = lax.optimization_barrier(partial_out.astype(jnp.bfloat16)).astype(jnp.float32)
    projected_out = lax.psum_scatter(
        rounded_out.astype(jnp.bfloat16), "chan", scatter_dimension=1, tiled=True
    ).astype(jnp.float32)
    return (tokens.astype(jnp.float32) + projected_out).astype(jnp.bfloat16)


def solution(mesh):
    in_specs = (
        P("seq", "chan"),
        P(),
        P("seq", None, "chan"),
        P(None, None, "chan"),
        P(None, "chan"),
        P("chan"),
        P("chan", None),
    )
    out_specs = P("seq", "chan")
    return jax.shard_map(
        per_device, mesh=mesh, in_specs=in_specs, out_specs=out_specs, check_vma=False
    )
```

profile of v0, /device:TPU:1, one launch (start us, length us, event | category | flops | bytes accessed | tf_op | source)
XLA Modules:
  0.0 403.7 jit_solution(17343954570505300916)
XLA Ops:
  6.5 0.0 copy-start
  6.5 0.0 all-gather.3.cloned.1.call-start
  6.5 0.7 all-gather.3.cloned.1.call-update
  7.3 0.0 all-gather.5.cloned.1.call-start
  7.3 2.3 copy.10
  9.6 0.0 all-gather.5.cloned.1.call-update
  9.6 0.0 reduce-scatter.2.cloned.1.call-start
  9.7 2.6 iota_compare_fusion
  12.3 0.0 copy-done
  12.3 9.2 %fusion.3 = f32[128,256,16]{1,2,0:T(8,128)} fusion(pred[128,128,256]{2,1,0:T(32,128)(4,1)S(1)} %iota_compare_fusion, f32[128,16]{0,1:T(8,128)S(1)} %copy-done), kind=kOutput, calls=%fused_computation.6 | convolution fusion | flops 805306368 | bytes 6299648 | tf_op jit(solution)/shard_map/jg,jis->gis/dot_general | solution.py:55
  21.5 77.9 %all-gather.3.cloned.1.call-done = bf16[512,8192]{1,0:T(8,128)(2,1)} async-done(((bf16[512,512]{1,0:T(8,128)(2,1)}), bf16[512,8192]{1,0:T(8,128)(2,1)}) %all-gather.3.cloned.1.call-update) | async-done | bytes 8388624 | tf_op jit(solution)/shard_map/all_gather | solution.py:26
  99.4 5.1 %fusion = f32[512]{0:T(512)S(1)} fusion(bf16[512,8192]{1,0:T(8,128)(2,1)} %all-gather.3.cloned.1.call-done), kind=kLoop, calls=%fused_computation.2 | loop fusion | flops 12582400 | bytes 8390656 | tf_op jit(solution)/shard_map/reduce_sum | solution.py:28
  104.5 137.9 %all-gather.5.cloned.1.call-done = bf16[8192,3,256]{0,2,1:T(8,128)(2,1)} async-done(((bf16[512,3,256]{0,2,1:T(8,128)(2,1)}), bf16[8192,3,256]{0,2,1:T(8,128)(2,1)}) %all-gather.5.cloned.1.call-update) | async-done | bytes 12582928 | tf_op jit(solution)/shard_map/all_gather | solution.py:30
  242.4 0.0 copy-done.5
  242.4 0.0 copy-start.4
  242.4 13.1 %fusion.14 = bf16[512,768]{1,0:T(8,128)(2,1)S(1)} fusion(bf16[8192,768]{0,1:T(8,128)(2,1)} %bitcast.50, bf16[512,8192]{1,0:T(8,128)(2,1)} %all-gather.3.cloned.1.call-done, f32[8192]{0:T(1024)S(1)} %copy-done.5, f32[512]{0:T(512)S(1)} %add_rsqrt_fusion), kind=kOutput, calls=%fused_computation.20 | convolution fusion | flops 6459621376 | bytes 21792768 | tf_op jit(solution)/shard_map/dot_general | solution.py:32
  255.6 1.3 collective-permute-start
  256.9 0.0 copy-done.4
  256.9 0.3 copy.11
  257.2 0.4 collective-permute-done
  257.6 0.2 copy.12
  257.8 0.5 pad_maximum_fusion
  258.3 0.1 convert_element_type.43
  258.5 1.4 fusion.12
  259.8 0.1 fusion.25
  259.9 0.1 slice_bitcast_fusion.1
  260.0 3.8 collective-permute-start.1
  263.8 0.1 fusion.33
  263.9 1.0 collective-permute-done.1
  264.9 0.2 pad_maximum_fusion.1
  265.1 0.1 slice.72
  265.3 0.2 pad_slice_fusion
  265.5 1.0 concatenate.20
  266.5 0.0 copy-start.3
  266.5 1.1 copy.15
  267.6 1.0 concatenate.21
  268.5 0.0 copy-start.1
  268.5 1.2 copy.16
  269.8 5.2 %fusion.17 = f32[4,128,16,16]{1,3,0,2:T(8,128)S(1)} fusion(f32[128,256,16]{1,2,0:T(8,128)} %fusion.3, f32[4,128,16,16]{1,3,0,2:T(8,128)S(1)} %copy.16, f32[4,128,16,16]{1,3,0,2:T(8,128)S(1)} %copy.15), kind=kOutput, calls=%fused_computation.21 | convolution fusion | flops 402915328 | bytes 3670016 | tf_op jit(solution)/shard_map/gis,bsgc->bigc/dot_general | solution.py:58
  274.9 0.2 copy.17
  275.1 0.0 copy-done.3
  275.1 0.0 copy-done.1
  275.2 5.9 %convolution_convert_fusion = bf16[512,8192]{1,0:T(8,128)(2,1)} fusion(bf16[256,8192]{1,0:T(8,128)(2,1)S(1)} %copy-done.1, f32[32,8,4,128]{3,2,1,0:T(4,128)S(1)} %bitcast.49, f32[512,3,256]{0,2,1:T(8,128)S(1)} %fusion.12, f32[256]{0:T(256)S(1)} %copy-done.3, f32[639,256]{0,1:T(8,128)S(1)} %convert_element_type.46), kind=kOutput, calls=%fused_computation.8 | convolution fusion | flops 2152202240 | bytes 14156800 | tf_op jit(solution)/shard_map/dot_general | solution.py:61
  281.1 0.0 copy-start.2
  281.1 0.0 reduce-scatter.2.cloned.1.call-update
  281.1 114.1 %reduce-scatter.2.cloned.1.call-done = bf16[512,512]{1,0:T(8,128)(2,1)} async-done(((bf16[512,8192]{1,0:T(8,128)(2,1)}), bf16[512,512]{1,0:T(8,128)(2,1)}) %reduce-scatter.2.cloned.1.call-update) | async-done | bytes 524304 | tf_op jit(solution)/shard_map/reduce_scatter | solution.py:63
  395.2 0.0 copy-done.2
  395.2 2.0 add_convert_fusion
  (7 shorter events, 0.1 us)
Async XLA Ops:
  6.5 5.8 %copy-start = (f32[128,16]{0,1:T(8,128)S(1)}, f32[128,16]{0,1:T(8,128)}, u32[]{:S(2)}) copy-start(f32[128,16]{0,1:T(8,128)} %param.11) | copy-start | bytes 24580
  6.5 92.8 %all-gather.3.cloned.1.call-start = ((), (), s32[]{:S(2)}) async-start(), calls=%async_computation.1 | async-start | bytes 8912896 | tf_op jit(solution)/shard_map/all_gather | solution.py:26
  7.3 235.2 %all-gather.5.cloned.1.call-start = ((), (), s32[]{:S(2)}) async-start(), calls=%async_computation.2 | async-start | bytes 13369344 | tf_op jit(solution)/shard_map/all_gather | solution.py:30
  9.6 385.6 %reduce-scatter.2.cloned.1.call-start = ((), (), s32[]{:S(2)}) async-start(), calls=%async_computation.3 | async-start | bytes 8912896 | tf_op jit(solution)/shard_map/reduce_scatter | solution.py:63
  21.5 220.9 %copy-start.5 = (f32[8192]{0:T(1024)S(1)}, f32[8192]{0:T(1024)}, u32[]{:S(2)}) copy-start(f32[8192]{0:T(1024)} %param.8) | copy-start | bytes 98308
  242.4 14.5 %copy-start.4 = (f32[3,3,256]{2,1,0:T(4,128)S(1)}, f32[3,3,256]{2,1,0:T(4,128)}, u32[]{:S(2)}) copy-start(f32[3,3,256]{2,1,0:T(4,128)} %param.10) | copy-start | bytes 27652
  255.6 2.0 collective-permute-start
  260.0 4.9 %collective-permute-start.1 = (bf16[127,256]{0,1:T(8,128)(2,1)S(1)}, bf16[127,256]{0,1:T(8,128)(2,1)S(1)}, u32[]{:S(2)}, u32[]{:S(2)}) collective-permute-start(bf16[127,256]{0,1:T(8,128)(2,1)S(1)} %slice_bitcast_fusion.1), channel_id=1, source_target_pairs={{0,16},{16,32},{32,48},{48,64},{64,80},{80,96},{96,112},{112,128},... | collective-permute-start | bytes 195080 | tf_op jit(solution)/shard_map/ppermute | solution.py:16
  266.5 8.7 %copy-start.3 = (f32[256]{0:T(256)S(1)}, f32[256]{0:T(256)}, u32[]{:S(2)}) copy-start(f32[256]{0:T(256)} %param.12) | copy-start | bytes 3076
  268.5 6.6 %copy-start.1 = (bf16[256,8192]{1,0:T(8,128)(2,1)S(1)}, bf16[256,8192]{1,0:T(8,128)(2,1)}, u32[]{:S(2)}) copy-start(bf16[256,8192]{1,0:T(8,128)(2,1)} %param.13) | copy-start | bytes 12582916
  281.1 114.1 %copy-start.2 = (bf16[512,512]{1,0:T(8,128)(2,1)S(1)}, bf16[512,512]{1,0:T(8,128)(2,1)}, u32[]{:S(2)}) copy-start(bf16[512,512]{1,0:T(8,128)(2,1)} %param.7) | copy-start | bytes 1572868
Sparse Core Ops, SparseCore 0:
  9.9 89.4 all-gather.2
  101.2 141.1 all-gather.4
  281.2 113.9 reduce-scatter.1
where the time goes:
time: 404 us
  waiting for transfers between devices  332 us (82%)
  matrix products  33.4 us (8%)
  between operations  13.3 us (3%)
  other arithmetic  12 us (3%)
  local copies, waits for them, and re-layouts  7.71 us (2%)
  starting transfers between devices  5.2 us (1%)
    all_gather x1, waiting for transfers between devices, per_device(): section = lax.all_gather(w_in, 'seq', axis=0, tiled=True)  138 us
    reduce_scatter x1, waiting for transfers between devices, per_device(): lax.psum_scatter(rounded_out.astype(jnp.bfloat16), 'chan', scatter_dimens...  114 us
    all_gather x1, waiting for transfers between devices, per_device(): gathered = lax.all_gather(tokens, 'chan', axis=1, tiled=True)  77.9 us
    dot_general x1, matrix products, per_device(): summed = jnp.dot(normed, flat_section, preferred_element_type=jnp.float32)  13.1 us
    dot_general x1, matrix products, per_device(): jnp.einsum('jg,jis->gis', medium_taps, onehot, precision=lax.Precision.HI...  9.22 us
  transfers between devices with their start and end apart: 5, of which 5 were waited for; matrix products, arithmetic and copies ran while one was open for 5% of the time, Pallas kernels for 0%

commit v1 on v0

--- a/solution.py
+++ b/solution.py
@@ -1,13 +1,331 @@
+import functools
 import jax
 import jax.numpy as jnp
 from jax import lax
+from jax.experimental import pallas as pl
+from jax.experimental.pallas import tpu as pltpu
 from jax.sharding import PartitionSpec as P
 
 TAPS = 128
 GROUP = 16
-
-
 EPSILON = 1e-06
+MESH = pl.DeviceIdType.MESH
+ROWS = 512
+WIDE = 512
+CH = 256
+F32 = jnp.float32
+BF16 = jnp.bfloat16
+
+
+def project_kernel(
+    x_hbm, gain_ref, w_hbm, out_ref,
+    tok, tg, wb, acc, cs, cr, sq, ss, sr,
+    loc, w_send, w_recv, y_send, y_recv, x_send, x_recv, d_send, d_recv, c_send, c_recv, s_send, s_recv,
+):
+    s = lax.axis_index("seq")
+    c = lax.axis_index("chan")
+    y_lo, z = s // 8, s % 8
+    y_hi, x, core = c // 8, (c // 2) % 4, c % 2
+    f_own = x * 2 + core
+    x_right, x_left, x_far = (x + 1) % 4, (x + 3) % 4, (x + 2) % 4
+
+    def at(y_hi_=y_hi, x_=x, core_=core, y_lo_=y_lo, z_=z):
+        return (y_lo_ * 8 + z_, y_hi_ * 8 + x_ * 2 + core_)
+
+    right, left = at(x_=x_right), at(x_=x_left)
+    up, down = at(z_=(z + 1) % 8), at(z_=(z + 7) % 8)
+    twin = at(core_=1 - core)
+    mate = at(y_lo_=1 - y_lo)
+    opposite = at(y_hi_=1 - y_hi)
+    diagonal = at(y_hi_=1 - y_hi, y_lo_=1 - y_lo)
+
+    def remote(src, dst, send, recv, device):
+        return pltpu.make_async_remote_copy(
+            src_ref=src, dst_ref=dst, send_sem=send, recv_sem=recv, device_id=device, device_id_type=MESH
+        )
+
+    own_w = [
+        pltpu.make_async_copy(w_hbm.at[:, pl.ds(h * 256, 256), :], wb.at[z, h], loc.at[h]) for h in range(2)
+    ]
+    for cp in own_w:
+        cp.start()
+
+    barrier = pltpu.get_barrier_semaphore()
+    peers = (right, left, up, down, twin, mate, opposite, diagonal)
+    for peer in peers:
+        pl.semaphore_signal(barrier, inc=1, device_id=peer, device_id_type=MESH)
+    pl.semaphore_wait(barrier, len(peers))
+
+    def w_slot(direction, distance, half, ahead=0):
+        source = (z + 8 - distance) % 8 if direction == 0 else (z + distance) % 8
+        return wb.at[source, half]
+
+    def recv_place(direction, k):
+        if k == 6:
+            return 4, direction
+        return k // 2 + 1, k % 2
+
+    def send_place(direction, k):
+        if k < 2:
+            return 0, k
+        if k == 6:
+            return 3, direction
+        return (k - 2) // 2 + 1, (k - 2) % 2
+
+    def w_copy(direction, k):
+        slot = w_slot(direction, *send_place(direction, k))
+        return remote(slot, slot, w_send.at[direction, k], w_recv.at[direction, k], up if direction == 0 else down)
+
+    def w_wait(direction, k):
+        slot = w_slot(direction, *recv_place(direction, k))
+        remote(slot, slot, w_send.at[direction, k], w_recv.at[direction, k], up).wait_recv()
+
+    for h in range(2):
+        own_w[h].wait()
+        for direction in range(2):
+            w_copy(direction, h).start()
+
+    is_home = y_hi == y_lo
+    def y_copy(d):
+        slot = tok.at[y_lo, f_own]
+        return remote(x_hbm, slot, y_send.at[d], y_recv.at[y_lo], at(y_lo_=y_hi, y_hi_=d))
+
+    own_x = pltpu.make_async_copy(x_hbm, tok.at[y_lo, f_own], loc.at[2])
+    for d in range(2):
+        stays = jnp.logical_and(is_home, y_hi == d)
+
+        @pl.when(jnp.logical_not(stays))
+        def _():
+            y_copy(d).start()
+
+        @pl.when(stays)
+        def _():
+            own_x.start()
+
+    def step(k):
+        for direction in range(2):
+            w_wait(direction, k - 2)
+            if k < 6:
+                w_copy(direction, k).start()
+
+    acc[...] = jnp.zeros_like(acc)
+    sq[...] = jnp.zeros_like(sq)
+
+    step(2)
+
+    for u in range(2):
+        stays = jnp.logical_and(is_home, y_lo == u)
+        slot = tok.at[u, f_own]
+
+        @pl.when(jnp.logical_not(stays))
+        def _():
+            remote(slot, slot, y_send.at[0], y_recv.at[u], right).wait_recv()
+
+        @pl.when(stays)
+        def _():
+            pltpu.make_async_copy(x_hbm, slot, loc.at[2]).wait()
+
+    def x_copy(direction, k):
+        device = right if direction == 0 else left
+        if k < 2:
+            u = k if direction == 0 else 1 - k
+            slot = tok.at[u, f_own]
+        else:
+            slot = tok.at[direction, (x_left if direction == 0 else x_right) * 2 + core]
+        return remote(slot, slot, x_send.at[direction, k], x_recv.at[direction, k], device)
+
+    def x_place(direction, k):
+        near = x_left if direction == 0 else x_right
+        if k < 2:
+            u = k if direction == 0 else 1 - k
+            return u, near
+        return direction, x_far
+
+    def x_wait(direction, k):
+        u, source = x_place(direction, k)
+        slot = tok.at[u, source * 2 + core]
+        remote(slot, slot, x_send.at[direction, k], x_recv.at[direction, k], right).wait_recv()
+
+    def d_copy(index, u, source, core_):
+        slot = tok.at[u, source * 2 + core_]
+        return remote(slot, slot, d_send.at[index], d_recv.at[index], twin)
+
+    places = [(0, x), (1, x)]
+    for k in range(3):
+        for direction in range(2):
+            places.append(x_place(direction, k))
+
+    for k in range(2):
+        for direction in range(2):
+            x_copy(direction, k).start()
+    for index in range(2):
+        d_copy(index, *places[index], core).start()
+
+    def scaled(u, f):
+        def body(i, carry):
+            rows = pl.ds(pl.multiple_of(i * 64, 64), 64)
+            raw = tok[u, f, rows, :].astype(F32)
+            gain = gain_ref[pl.ds(y_lo * 8 + f, 1), 0, :]
+            tg[u, f, rows, :] = (raw * gain).astype(BF16)
+            square = raw * raw
+            total = square[:, 0:128] + square[:, 128:256] + square[:, 256:384] + square[:, 384:512]
+            sq[u, rows, :] += total
+            return carry
+
+        lax.fori_loop(0, 8, body, 0)
+
+    def taken(index):
+        u, source = places[index]
+        scaled(u, source * 2 + core)
+        d_copy(index, u, source, 1 - core).wait_recv()
+        scaled(u, source * 2 + 1 - core)
+
+    step(3)
+    taken(0)
+    taken(1)
+    step(4)
+    for direction in range(2):
+        x_wait(direction, 0)
+        x_copy(direction, 2).start()
+        d_copy(2 + direction, *places[2 + direction], core).start()
+    step(5)
+    for direction in range(2):
+        x_wait(direction, 1)
+        d_copy(4 + direction, *places[4 + direction], core).start()
+    for index in range(2, 6):
+        taken(index)
+    for direction in range(2):
+        w_wait(direction, 4)
+        w_wait_other = None
+        if direction == 0:
+            w_copy(0, 6).start()
+    for direction in range(2):
+        w_wait(direction, 5)
+        if direction == 1:
+            w_copy(1, 6).start()
+    for direction in range(2):
+        x_wait(direction, 2)
+        d_copy(6 + direction, *places[6 + direction], core).start()
+    for index in range(6, 8):
+        taken(index)
+
+    other = 1 - y_lo
+
+    def row_sums(u):
+        column = jnp.sum(sq[u], axis=1, keepdims=True)
+        return jnp.transpose(jnp.broadcast_to(column, (ROWS, 128)))[0:8, :]
+
+    ss[...] = row_sums(other)
+    s_copy = remote(ss, sr, s_send, s_recv, mate)
+    s_copy.start()
+
+    def multiply(u, f, i):
+        rows = pl.ds(pl.multiple_of(i * 256, 256), 256)
+        lhs0 = tg[u, f, rows, 0:256]
+        lhs1 = tg[u, f, rows, 256:512]
+        parts = []
+        for p in range(3):
+            part = jnp.dot(lhs0, wb[f, 0, p], preferred_element_type=F32)
+            part += jnp.dot(lhs1, wb[f, 1, p], preferred_element_type=F32)
+            parts.append(part)
+        return rows, parts
+
+    def add_chunk(f):
+        def body(i, carry):
+            u, i = i // 2, i % 2
+            rows, parts = multiply(u, f, i)
+            for p in range(3):
+                acc[u, p, rows, :] += parts[p]
+            return carry
+
+        lax.fori_loop(0, 4, body, 0)
+
+    def chunk_loop(j, carry):
+        add_chunk((z + 5 + j) % 8)
+        return carry
+
+    lax.fori_loop(0, 7, chunk_loop, 0)
+    for direction in range(2):
+        w_wait(direction, 6)
+    f_last = (z + 4) % 8
+
+    def c_copy(i):
+        rows = pl.ds(i * 256, 256)
+        return remote(cs.at[:, rows, :], cr.at[:, rows, :], c_send.at[i], c_recv.at[i], mate)
+
+    for i in (1, 0):
+        rows, parts = multiply(other, f_last, i)
+        for p in range(3):
+            cs[p, rows, :] = (acc[other, p, rows, :] + parts[p]).astype(BF16)
+        c_copy(i).start()
+
+    s_copy.wait()
+    total = row_sums(y_lo) + sr[...]
+    factor = lax.rsqrt(total * (1.0 / 8192.0) + EPSILON)
+    factor = jnp.transpose(jnp.broadcast_to(factor[0:1, :], (128, ROWS)))
+    sq[0] = factor
+    for i in (1, 0):
+        rows, parts = multiply(y_lo, f_last, i)
+        for p in range(3):
+            acc[y_lo, p, rows, :] += parts[p]
+    for i in (1, 0):
+        rows = pl.ds(i * 256, 256)
+        c_copy(i).wait_recv()
+        factor = sq[0, rows, :]
+        factor = jnp.concatenate([factor, factor], axis=1)
+        for p in range(3):
+            value = acc[y_lo, p, rows, :] + cr[p, rows, :].astype(F32)
+            out_ref[p, rows, :] = (value * factor).astype(BF16)
+
+    for direction in range(2):
+        for k in range(7):
+            w_copy(direction, k).wait_send()
+        for k in range(3):
+            x_copy(direction, k).wait_send()
+    for d in range(2):
+        @pl.when(jnp.logical_not(jnp.logical_and(is_home, y_hi == d)))
+        def _():
+            y_copy(d).wait_send()
+    for index in range(8):
+        d_copy(index, *places[index], core).wait_send()
+    for i in range(2):
+        c_copy(i).wait_send()
+
+
+def project(tokens, gain, w_planes):
+    dma = pltpu.SemaphoreType.DMA
+    return pl.pallas_call(
+        project_kernel,
+        out_shape=jax.ShapeDtypeStruct((3, ROWS, CH), BF16),
+        in_specs=[
+            pl.BlockSpec(memory_space=pl.ANY),
+            pl.BlockSpec(memory_space=pltpu.VMEM),
+            pl.BlockSpec(memory_space=pl.ANY),
+        ],
+        out_specs=pl.BlockSpec(memory_space=pltpu.VMEM),
+        scratch_shapes=[
+            pltpu.VMEM((2, 8, ROWS, WIDE), BF16),
+            pltpu.VMEM((2, 8, ROWS, WIDE), BF16),
+            pltpu.VMEM((8, 2, 3, 256, CH), BF16),
+            pltpu.VMEM((2, 3, ROWS, CH), F32),
+            pltpu.VMEM((3, ROWS, CH), BF16),
+            pltpu.VMEM((3, ROWS, CH), BF16),
+            pltpu.VMEM((2, ROWS, 128), F32),
+            pltpu.VMEM((8, ROWS), F32),
+            pltpu.VMEM((8, ROWS), F32),
+            dma((3,)),
+            dma((2, 7)), dma((2, 7)),
+            dma((2,)), dma((2,)),
+            dma((2, 3)), dma((2, 3)),
+            dma((8,)), dma((8,)),
+            dma((2,)), dma((2,)),
+            dma, dma,
+        ],
+        compiler_params=pltpu.CompilerParams(
+            collective_id=0, has_side_effects=True, vmem_limit_bytes=56 * 1024 * 1024
+        ),
+        name="project",
+    )(tokens, gain, w_planes)
 
 
 def passed_along(value, axis, steps):
@@ -23,14 +341,8 @@
 def per_device(tokens, norm_gain, w_in, short_taps, medium_taps, skip_gain, w_out):
     row_count = tokens.shape[0]
     channels = w_in.shape[2]
-    gathered = lax.all_gather(tokens, "chan", axis=1, tiled=True)
-    widened = gathered.astype(jnp.float32)
-    mean_square = jnp.mean(widened * widened, axis=1, keepdims=True)
-    normed = (widened * lax.rsqrt(mean_square + EPSILON) * norm_gain).astype(jnp.bfloat16)
-    section = lax.all_gather(w_in, "seq", axis=0, tiled=True)
-    flat_section = section.reshape(section.shape[0], 3 * channels)
-    summed = jnp.dot(normed, flat_section, preferred_element_type=jnp.float32)
-    projected = summed.astype(jnp.bfloat16).reshape(row_count, 3, channels)
+    planes = project(tokens, norm_gain.reshape(16, 1, WIDE), jnp.transpose(w_in, (1, 0, 2)))
+    projected = jnp.transpose(planes, (1, 0, 2))
     edge_rows = passed_along(projected[row_count - 2 :], "seq", 1)
     extended = lax.optimization_barrier(jnp.concatenate([edge_rows, projected], 0)).astype(
         jnp.float32

time: 404 us -> 266 us (0.66)
  waiting for transfers between devices: 332 us -> 111 us
  Pallas kernels: 0 us -> 102 us
  matrix products: 33.4 us -> 22 us
  other arithmetic: 12 us -> 5.53 us
    all_gather x2 -> x0, waiting for transfers between devices: 216 us -> none  [the longest x1 138 us: per_device(): section = lax.all_gather(w_in, 'seq', axis=0, tiled=True)]
    pallas_call x0 -> x1, Pallas kernels: none -> 102 us  [project(): pl.pallas_call(project_kernel, out_shape=jax.ShapeDtypeStruct((3, ROWS, C...]
    dot_general x1 -> x0, matrix products: 13.1 us -> none  [per_device(): summed = jnp.dot(normed, flat_section, preferred_element_type=jnp.float32)]
    reduce_sum x1 -> x0, other arithmetic: 5.1 us -> none  [per_device(): mean_square = jnp.mean(widened * widened, axis=1, keepdims=True)]
    reduce_scatter x1, waiting for transfers between devices: 114 us -> 109 us  [per_device(): lax.psum_scatter(rounded_out.astype(jnp.bfloat16), 'chan', scatter_dimens...]
  transfers between devices with their start and end apart: 5 -> 3, of which waited for: 5 -> 2; matrix products, arithmetic and copies ran while one was open for 5% -> 4% of each run, Pallas kernels for 0% -> 0%
where the time goes in v1:
time: 266 us
  waiting for transfers between devices  111 us (42%)
  Pallas kernels  102 us (38%)
  matrix products  22 us (8%)
  between operations  13.6 us (5%)
  local copies, waits for them, and re-layouts  7.8 us (3%)
  other arithmetic  5.53 us (2%)
  starting transfers between devices  3.54 us (1%)
    reduce_scatter x1, waiting for transfers between devices, per_device(): lax.psum_scatter(rounded_out.astype(jnp.bfloat16), 'chan', scatter_dimens...  109 us
    pallas_call x1, Pallas kernels, project(): pl.pallas_call(project_kernel, out_shape=jax.ShapeDtypeStruct((3, ROWS, C...  102 us
    dot_general x1, matrix products, per_device(): jnp.einsum('jg,jis->gis', medium_taps, onehot, precision=lax.Precision.HI...  9.24 us
    dot_general x1, matrix products, per_device(): partial_out = jnp.dot(gating, w_out, preferred_element_type=jnp.float32)  7.8 us
  transfers between devices with their start and end apart: 3, of which 2 were waited for; matrix products, arithmetic and copies ran while one was open for 4% of the time, Pallas kernels for 0%

profile of v1, /device:TPU:1, one launch (start us, length us, event | category | flops | bytes accessed | tf_op | source)
XLA Modules:
  0.0 265.8 jit_solution(7203355126731754416)
XLA Ops:
  6.5 0.0 copy-start
  6.5 0.0 reduce-scatter.2.cloned.1.call-start
  6.5 102.5 %project.1 = bf16[3,512,256]{2,1,0:T(8,128)(2,1)} custom-call(bf16[512,512]{1,0:T(8,128)(2,1)} %x_hbm.1, f32[16,1,512]{2,1,0:T(1,128)} %bitcast.51, bf16[3,512,256]{2,1,0:T(8,128)(2,1)} %bitcast.50), custom_call_target="tpu_custom_call" | custom-call | tf_op jit(solution)/shard_map/project/pallas_call | solution.py:297
  109.0 0.7 slice.60
  109.7 1.5 collective-permute-start
  111.2 2.6 iota_compare_fusion
  113.8 0.0 copy-done
  113.8 0.0 copy-start.4
  113.8 0.0 copy-start.1
  113.8 9.2 %fusion = f32[128,256,16]{1,2,0:T(8,128)} fusion(pred[128,128,256]{2,1,0:T(32,128)(4,1)S(1)} %iota_compare_fusion, f32[128,16]{0,1:T(8,128)S(1)} %copy-done), kind=kOutput, calls=%fused_computation.1 | convolution fusion | flops 805306368 | bytes 6299648 | tf_op jit(solution)/shard_map/jg,jis->gis/dot_general | solution.py:367
  123.0 0.0 copy-done.4
  123.0 0.0 collective-permute-done
  123.1 0.0 copy-done.1
  123.1 0.2 pad_maximum_fusion
  123.3 0.1 convert_element_type.31
  123.4 0.5 fusion.5
  123.9 0.1 fusion.13
  123.9 2.1 collective-permute-start.1
  126.0 0.1 fusion.22
  126.1 1.4 collective-permute-done.1
  127.5 0.1 pad_maximum_fusion.1
  127.5 0.1 slice.68
  127.7 0.2 copy.12
  127.9 1.0 concatenate.21
  128.8 1.1 copy.14
  129.9 0.8 pad_slice_fusion
  130.7 1.2 copy.11
  132.0 1.0 concatenate.20
  132.9 1.1 copy.13
  134.0 5.0 %fusion.7 = f32[4,128,16,16]{1,3,0,2:T(8,128)S(1)} fusion(f32[128,256,16]{1,2,0:T(8,128)} %fusion, f32[4,128,16,16]{1,3,0,2:T(8,128)S(1)} %copy.14, f32[4,128,16,16]{1,3,0,2:T(8,128)S(1)} %copy.13), kind=kOutput, calls=%fused_computation.12 | convolution fusion | flops 402915328 | bytes 3670016 | tf_op jit(solution)/shard_map/gis,bsgc->bigc/dot_general | solution.py:370
  139.0 0.0 copy-start.3
  139.0 0.2 copy.15
  139.3 0.2 copy.16
  139.5 0.2 copy-done.3
  139.7 7.8 %convolution_convert_fusion = bf16[512,8192]{1,0:T(8,128)(2,1)} fusion(bf16[256,8192]{1,0:T(8,128)(2,1)} %param.13, f32[512,3,256]{2,0,1:T(8,128)S(1)} %fusion.5, f32[512,256]{1,0:T(8,128)S(1)} %copy.16, f32[256]{0:T(256)S(1)} %copy-done.3, f32[639,256]{1,0:T(8,128)S(1)} %convert_element_type.34), kind=kOutput, calls=%fused_computation.3 | convolution fusion | flops 2152202240 | bytes 14156800 | tf_op jit(solution)/shard_map/dot_general | solution.py:373
  147.5 0.0 copy-start.2
  147.5 0.0 reduce-scatter.2.cloned.1.call-update
  147.5 109.5 %reduce-scatter.2.cloned.1.call-done = bf16[512,512]{1,0:T(8,128)(2,1)} async-done(((bf16[512,8192]{1,0:T(8,128)(2,1)}), bf16[512,512]{1,0:T(8,128)(2,1)}) %reduce-scatter.2.cloned.1.call-update) | async-done | bytes 524304 | tf_op jit(solution)/shard_map/reduce_scatter | solution.py:375
  257.0 0.0 copy-done.2
  257.0 2.0 add_convert_fusion
  (5 shorter events, 0.1 us)
Async XLA Ops:
  6.5 107.2 %copy-start = (f32[128,16]{0,1:T(8,128)S(1)}, f32[128,16]{0,1:T(8,128)}, u32[]{:S(2)}) copy-start(f32[128,16]{0,1:T(8,128)} %param.11) | copy-start | bytes 24580
  6.5 250.5 %reduce-scatter.2.cloned.1.call-start = ((), (), s32[]{:S(2)}) async-start(), calls=%async_computation.1 | async-start | bytes 8912896 | tf_op jit(solution)/shard_map/reduce_scatter | solution.py:375
  109.7 13.3 %collective-permute-start = (bf16[2,3,256]{2,0,1:T(2,128)(2,1)S(1)}, bf16[2,3,256]{2,0,1:T(2,128)(2,1)S(1)}, u32[]{:S(2)}, u32[]{:S(2)}) collective-permute-start(bf16[2,3,256]{2,0,1:T(2,128)(2,1)S(1)} %slice.60), channel_id=1, source_target_pairs={{0,16},{16,32},{32,48},{48,64},{64,80},{80,96},{96,112},{112,128},... | collective-permute-start | bytes 9224 | tf_op jit(solution)/shard_map/ppermute | solution.py:334
  113.8 9.3 %copy-start.4 = (f32[3,3,256]{2,1,0:T(4,128)S(1)}, f32[3,3,256]{2,1,0:T(4,128)}, u32[]{:S(2)}) copy-start(f32[3,3,256]{2,1,0:T(4,128)} %param.10) | copy-start | bytes 27652
  113.8 9.3 %copy-start.1 = (bf16[3,512,256]{2,1,0:T(8,128)(2,1)S(1)}, bf16[3,512,256]{2,1,0:T(8,128)(2,1)}, u32[]{:S(2)}) copy-start(bf16[3,512,256]{2,1,0:T(8,128)(2,1)} %project.1) | copy-start | bytes 2359300
  123.9 3.5 %collective-permute-start.1 = (bf16[127,256]{1,0:T(8,128)(2,1)S(1)}, bf16[127,256]{1,0:T(8,128)(2,1)S(1)}, u32[]{:S(2)}, u32[]{:S(2)}) collective-permute-start(bf16[127,256]{1,0:T(8,128)(2,1)S(1)} %slice_bitcast_fusion.1), channel_id=1, source_target_pairs={{0,16},{16,32},{32,48},{48,64},{64,80},{80,96},{96,112},{112,128},... | collective-permute-start | bytes 195080 | tf_op jit(solution)/shard_map/ppermute | solution.py:334
  139.0 0.7 copy-start.3
  147.5 109.5 %copy-start.2 = (bf16[512,512]{1,0:T(8,128)(2,1)S(1)}, bf16[512,512]{1,0:T(8,128)(2,1)}, u32[]{:S(2)}) copy-start(bf16[512,512]{1,0:T(8,128)(2,1)} %x_hbm.1) | copy-start | bytes 1572868
Sparse Core Ops, SparseCore 0:
  147.6 109.3 reduce-scatter.1

commit v2 on v1

--- a/solution.py
+++ b/solution.py
@@ -1,4 +1,3 @@
-import functools
 import jax
 import jax.numpy as jnp
 from jax import lax
@@ -17,10 +16,11 @@
 BF16 = jnp.bfloat16
 
 
-def project_kernel(
-    x_hbm, gain_ref, w_hbm, out_ref,
-    tok, tg, wb, acc, cs, cr, sq, ss, sr,
+def block_kernel(
+    x_hbm, gain_ref, w_hbm, short_ref, taps_ref, skip_ref, wo_hbm, out_ref,
+    tok, tg, wb, acc, cs, cr, sq, ss, sr, wo, toep, pj, pe, gate, sb, rb, yb, yr, xres,
     loc, w_send, w_recv, y_send, y_recv, x_send, x_recv, d_send, d_recv, c_send, c_recv, s_send, s_recv,
+    o_loc, o_send, o_recv, h_send, h_recv, g_send, g_recv, r_send, r_recv, v_send, v_recv,
 ):
     s = lax.axis_index("seq")
     c = lax.axis_index("chan")
@@ -38,6 +38,7 @@
     mate = at(y_lo_=1 - y_lo)
     opposite = at(y_hi_=1 - y_hi)
     diagonal = at(y_hi_=1 - y_hi, y_lo_=1 - y_lo)
+    after, before = ((s + 1) % 16, c), ((s + 15) % 16, c)
 
     def remote(src, dst, send, recv, device):
         return pltpu.make_async_remote_copy(
@@ -51,7 +52,7 @@
         cp.start()
 
     barrier = pltpu.get_barrier_semaphore()
-    peers = (right, left, up, down, twin, mate, opposite, diagonal)
+    peers = (right, left, up, down, twin, mate, opposite, diagonal, after, before)
     for peer in peers:
         pl.semaphore_signal(barrier, inc=1, device_id=peer, device_id_type=MESH)
     pl.semaphore_wait(barrier, len(peers))
@@ -108,8 +109,35 @@
             if k < 6:
                 w_copy(direction, k).start()
 
+    def columns(d, core_):
+        return wo_hbm.at[:, pl.ds(pl.multiple_of((d * 2 + core_) * WIDE, WIDE), WIDE)]
+
+    def o_keep(d):
+        return pltpu.make_async_copy(columns(d, core), wo.at[core, d], o_loc.at[d])
+
+    def o_copy(d):
+        return remote(columns(d, 1 - core), wo.at[core, d], o_send.at[d], o_recv.at[d], twin)
+
+    for d in range(8):
+        o_copy(d).start()
+        o_keep(d).start()
+    keep_x = pltpu.make_async_copy(x_hbm, xres, loc.at[3])
+    keep_x.start()
+
     acc[...] = jnp.zeros_like(acc)
     sq[...] = jnp.zeros_like(sq)
+
+    spread = (
+        lax.broadcasted_iota(jnp.int32, (TAPS, 2 * TAPS), 0) + lax.broadcasted_iota(jnp.int32, (TAPS, 2 * TAPS), 1)
+        == TAPS
+    ).astype(F32)
+    first = jnp.dot(taps_ref[...], spread, precision=lax.Precision.HIGHEST, preferred_element_type=F32)
+    for g in range(16):
+        row = jnp.broadcast_to(first[g : g + 1, :], (TAPS, 2 * TAPS))
+        matrix = pltpu.roll(row, 0, 1, stride=1, stride_axis=0)
+        high = matrix.astype(BF16)
+        toep[0, g] = high
+        toep[1, g] = (matrix - high.astype(F32)).astype(BF16)
 
     step(2)
 
@@ -268,14 +296,147 @@
         rows, parts = multiply(y_lo, f_last, i)
         for p in range(3):
             acc[y_lo, p, rows, :] += parts[p]
-    for i in (1, 0):
+    def finish(i):
         rows = pl.ds(i * 256, 256)
         c_copy(i).wait_recv()
         factor = sq[0, rows, :]
         factor = jnp.concatenate([factor, factor], axis=1)
         for p in range(3):
             value = acc[y_lo, p, rows, :] + cr[p, rows, :].astype(F32)
-            out_ref[p, rows, :] = (value * factor).astype(BF16)
+            pj[p, pl.ds(16 + i * 256, 256), :] = (value * factor).astype(BF16)
+
+    def filtered(p, r):
+        extended = pj[p, pl.ds(r * 128, 144), :].astype(F32)
+        taps = [short_ref[k, pl.ds(p, 1), :] for k in range(3)]
+        return taps[0] * extended[16:144] + taps[1] * extended[15:143] + taps[2] * extended[14:142]
+
+    def make_product(r):
+        pe[pl.ds(128 + r * 128, 128), :] = (filtered(1, r) * filtered(2, r)).astype(BF16)
+
+    halo_out = [
+        remote(pe.at[pl.ds(512, 128), :], pe.at[pl.ds(0, 128), :], h_send.at[0], h_recv.at[0], after),
+        remote(pj.at[:, pl.ds(512, 16), :], pj.at[:, pl.ds(0, 16), :], h_send.at[1], h_recv.at[1], after),
+    ]
+
+    group_of_lane = lax.broadcasted_iota(jnp.int32, (128, CH), 1) // GROUP
+
+    def g_copy(r):
+        place = gate.at[core, pl.ds(r * 128, 128), :]
+        return remote(place, place, g_send.at[r], g_recv.at[r], twin)
+
+    def make_gating(r):
+        window = pe[pl.ds(r * 128, 256), :]
+
+        def body(g, mixed):
+            part = jnp.dot(toep[0, g], window, preferred_element_type=F32)
+            part += jnp.dot(toep[1, g], window, preferred_element_type=F32)
+            return jnp.where(group_of_lane == g, part, mixed)
+
+        mixed = lax.fori_loop(0, 16, body, jnp.zeros((128, CH), F32), unroll=4)
+        product = pe[pl.ds(128 + r * 128, 128), :].astype(F32)
+        mixing = skip_ref[...] * product + mixed
+        gate[core, pl.ds(r * 128, 128), :] = (filtered(0, r) * mixing).astype(BF16)
+        g_copy(r).start()
+
+    def block(r, x_, y_hi_):
+        d = y_hi_ * 4 + x_
+        rows = pl.ds(r * 128, 128)
+        part = jnp.dot(gate[0, rows, :], wo[0, d], preferred_element_type=F32)
+        return part + jnp.dot(gate[1, rows, :], wo[1, d], preferred_element_type=F32)
+
+    def r_copy(r, direction, k):
+        return remote(
+            sb.at[r, direction, k], rb.at[r, direction, k], r_send.at[r, direction, k], r_recv.at[r, direction, k],
+            right if direction == 0 else left,
+        )
+
+    def v_copy(r):
+        return remote(yb.at[r], yr.at[r], v_send.at[r], v_recv.at[r], opposite)
+
+    nears = (x_right, x_left)
+
+    def send_first(r):
+        twin_place = gate.at[1 - core, pl.ds(r * 128, 128), :]
+        remote(twin_place, twin_place, g_send.at[r], g_recv.at[r], twin).wait_recv()
+        for direction in range(2):
+            sb[r, direction, 0] = block(r, x_far, direction).astype(BF16)
+            r_copy(r, direction, 0).start()
+        for direction in range(2):
+            sb[r, direction, 1] = block(r, nears[direction], 1 - direction).astype(BF16)
+            r_copy(r, direction, 1).start()
+
+    def send_joined(r):
+        for direction in range(2):
+            mine = block(r, nears[direction], direction)
+            r_copy(r, direction, 0).wait_recv()
+            sb[r, direction, 2] = (mine + rb[r, direction, 0].astype(F32)).astype(BF16)
+            r_copy(r, direction, 2).start()
+
+    def summed(r, y_hi_):
+        mine = block(r, x, y_hi_)
+        alone, joined = rb[r, 1 - y_hi_, 1], rb[r, y_hi_, 2]
+        return mine + alone.astype(F32) + joined.astype(F32)
+
+    def send_across(r):
+        for direction in range(2):
+            r_copy(r, direction, 1).wait_recv()
+            r_copy(r, direction, 2).wait_recv()
+        yb[r] = summed(r, 1 - y_hi).astype(BF16)
+        v_copy(r).start()
+
+    def write(r):
+        rows = pl.ds(r * 128, 128)
+        mine = summed(r, y_hi) + xres[rows, :].astype(F32)
+        v_copy(r).wait_recv()
+        out_ref[rows, :] = (mine + yr[r].astype(F32)).astype(BF16)
+
+    finish(1)
+    make_product(3)
+
+    @pl.when(s < 15)
+    def _():
+        for cp in halo_out:
+            cp.start()
+
+    @pl.when(s == 0)
+    def _():
+        pe[pl.ds(0, 128), :] = jnp.zeros((128, CH), BF16)
+        pj[:, pl.ds(0, 16), :] = jnp.zeros((3, 16, CH), BF16)
+
+    finish(0)
+    make_product(2)
+    for d in range(8):
+        o_keep(d).wait()
+        remote(wo.at[1 - core, d], wo.at[1 - core, d], o_send.at[d], o_recv.at[d], twin).wait_recv()
+    keep_x.wait()
+    make_gating(3)
+    make_product(1)
+    send_first(3)
+    make_gating(2)
+    send_first(2)
+
+    @pl.when(s > 0)
+    def _():
+        for cp in halo_out:
+            cp.wait_recv()
+
+    make_product(0)
+    make_gating(1)
+    send_joined(3)
+    send_first(1)
+    make_gating(0)
+    send_joined(2)
+    send_first(0)
+    send_across(3)
+    send_joined(1)
+    send_across(2)
+    write(3)
+    send_joined(0)
+    send_across(1)
+    write(2)
+    send_across(0)
+    write(1)
+    write(0)
 
     for direction in range(2):
         for k in range(7):
@@ -290,19 +451,30 @@
         d_copy(index, *places[index], core).wait_send()
     for i in range(2):
         c_copy(i).wait_send()
-
-
-def project(tokens, gain, w_planes):
+    for d in range(8):
+        o_copy(d).wait_send()
+    for r in range(4):
+        g_copy(r).wait_send()
+        v_copy(r).wait_send()
+        for direction in range(2):
+            for k in range(3):
+                r_copy(r, direction, k).wait_send()
+
+    @pl.when(s < 15)
+    def _():
+        for cp in halo_out:
+            cp.wait_send()
+
+
+def block_call(tokens, gain, w_planes, short_taps, taps, skip, w_out):
     dma = pltpu.SemaphoreType.DMA
+    vmem = pl.BlockSpec(memory_space=pltpu.VMEM)
+    far = pl.BlockSpec(memory_space=pl.ANY)
     return pl.pallas_call(
-        project_kernel,
-        out_shape=jax.ShapeDtypeStruct((3, ROWS, CH), BF16),
-        in_specs=[
-            pl.BlockSpec(memory_space=pl.ANY),
-            pl.BlockSpec(memory_space=pltpu.VMEM),
-            pl.BlockSpec(memory_space=pl.ANY),
-        ],
-        out_specs=pl.BlockSpec(memory_space=pltpu.VMEM),
+        block_kernel,
+        out_shape=jax.ShapeDtypeStruct((ROWS, WIDE), BF16),
+        in_specs=[far, vmem, far, vmem, vmem, vmem, far],
+        out_specs=vmem,
         scratch_shapes=[
             pltpu.VMEM((2, 8, ROWS, WIDE), BF16),
             pltpu.VMEM((2, 8, ROWS, WIDE), BF16),
@@ -313,69 +485,46 @@
             pltpu.VMEM((2, ROWS, 128), F32),
             pltpu.VMEM((8, ROWS), F32),
             pltpu.VMEM((8, ROWS), F32),
-            dma((3,)),
+            pltpu.VMEM((2, 8, CH, WIDE), BF16),
+            pltpu.VMEM((2, 16, TAPS, 2 * TAPS), BF16),
+            pltpu.VMEM((3, 16 + ROWS, CH), BF16),
+            pltpu.VMEM((128 + ROWS, CH), BF16),
+            pltpu.VMEM((2, ROWS, CH), BF16),
+            pltpu.VMEM((4, 2, 3, 128, WIDE), BF16),
+            pltpu.VMEM((4, 2, 3, 128, WIDE), BF16),
+            pltpu.VMEM((4, 128, WIDE), BF16),
+            pltpu.VMEM((4, 128, WIDE), BF16),
+            pltpu.VMEM((ROWS, WIDE), BF16),
+            dma((4,)),
             dma((2, 7)), dma((2, 7)),
             dma((2,)), dma((2,)),
             dma((2, 3)), dma((2, 3)),
             dma((8,)), dma((8,)),
             dma((2,)), dma((2,)),
             dma, dma,
+            dma((8,)), dma((8,)), dma((8,)),
+            dma((2,)), dma((2,)),
+            dma((4,)), dma((4,)),
+            dma((4, 2, 3)), dma((4, 2, 3)),
+            dma((4,)), dma((4,)),
         ],
         compiler_params=pltpu.CompilerParams(
-            collective_id=0, has_side_effects=True, vmem_limit_bytes=56 * 1024 * 1024
+            collective_id=0, has_side_effects=True, vmem_limit_bytes=58 * 1024 * 1024
         ),
-        name="project",
-    )(tokens, gain, w_planes)
-
-
-def passed_along(value, axis, steps):
-    count = lax.axis_size(axis)
-    first, last = (max(0, -steps), min(count, count - steps))
-    return lax.ppermute(value, axis, [(source, source + steps) for source in range(first, last)])
-
-
-def short_filter(extended, taps):
-    return taps[0] * extended[2:] + taps[1] * extended[1:-1] + taps[2] * extended[:-2]
+        name="block",
+    )(tokens, gain, w_planes, short_taps, taps, skip, w_out)
 
 
 def per_device(tokens, norm_gain, w_in, short_taps, medium_taps, skip_gain, w_out):
-    row_count = tokens.shape[0]
-    channels = w_in.shape[2]
-    planes = project(tokens, norm_gain.reshape(16, 1, WIDE), jnp.transpose(w_in, (1, 0, 2)))
-    projected = jnp.transpose(planes, (1, 0, 2))
-    edge_rows = passed_along(projected[row_count - 2 :], "seq", 1)
-    extended = lax.optimization_barrier(jnp.concatenate([edge_rows, projected], 0)).astype(
-        jnp.float32
+    return block_call(
+        tokens,
+        norm_gain.reshape(16, 1, WIDE),
+        jnp.transpose(w_in, (1, 0, 2)),
+        short_taps,
+        jnp.transpose(medium_taps),
+        skip_gain.reshape(1, CH),
+        w_out,
     )
-    filtered = short_filter(extended, short_taps)
-    queries = filtered[:, 0]
-    product = (filtered[:, 1] * filtered[:, 2]).astype(jnp.bfloat16)
-    product_rows = passed_along(product[row_count - (TAPS - 1) :], "seq", 1)
-    reached = jnp.concatenate([product_rows, product], 0)
-    floats = lax.optimization_barrier(reached).astype(jnp.float32)
-    padded = jnp.concatenate([jnp.zeros((1, channels), jnp.float32), floats], 0)
-    block_count = row_count // TAPS
-    blocks = padded.reshape(block_count + 1, TAPS, channels)
-    windows = jnp.concatenate([blocks[:-1], blocks[1:]], 1)
-    cube_shape = (TAPS, TAPS, 2 * TAPS)
-    lagged = (
-        lax.broadcasted_iota(jnp.int32, cube_shape, 1)
-        + TAPS
-        - lax.broadcasted_iota(jnp.int32, cube_shape, 2)
-    )
-    onehot = (lagged == lax.broadcasted_iota(jnp.int32, cube_shape, 0)).astype(jnp.float32)
-    toeplitz = jnp.einsum("jg,jis->gis", medium_taps, onehot, precision=lax.Precision.HIGHEST)
-    filters = medium_taps.shape[1]
-    grouped = windows.reshape(block_count, 2 * TAPS, filters, GROUP)
-    convolved = jnp.einsum("gis,bsgc->bigc", toeplitz, grouped, precision=lax.Precision.HIGHEST)
-    mixing = skip_gain * floats[TAPS - 1 :] + convolved.reshape(row_count, channels)
-    gating = (queries * mixing).astype(jnp.bfloat16)
-    partial_out = jnp.dot(gating, w_out, preferred_element_type=jnp.float32)
-    rounded_out = lax.optimization_barrier(partial_out.astype(jnp.bfloat16)).astype(jnp.float32)
-    projected_out = lax.psum_scatter(
-        rounded_out.astype(jnp.bfloat16), "chan", scatter_dimension=1, tiled=True
-    ).astype(jnp.float32)
-    return (tokens.astype(jnp.float32) + projected_out).astype(jnp.bfloat16)
 
 
 def solution(mesh):

time: 266 us -> 148 us (0.56)
  waiting for transfers between devices: 111 us -> 0 us
  Pallas kernels: 102 us -> 145 us
  matrix products: 22 us -> 0 us
  between operations: 13.6 us -> 0.01 us
  local copies, waits for them, and re-layouts: 7.8 us -> 1.87 us
  other arithmetic: 5.53 us -> 0 us
  starting transfers between devices: 3.54 us -> 0 us
    reduce_scatter x1 -> x0, waiting for transfers between devices: 109 us -> none  [per_device(): lax.psum_scatter(rounded_out.astype(jnp.bfloat16), 'chan', scatter_dimens...]
    pallas_call x1, Pallas kernels: 102 us -> 145 us  [block_call(): pl.pallas_call(block_kernel, out_shape=jax.ShapeDtypeStruct((ROWS, WIDE),...]
    dot_general x3 -> x0, matrix products: 22 us -> none  [the longest x1 9.24 us: per_device(): jnp.einsum('jg,jis->gis', medium_taps, onehot, precision=lax.Precision.HI...]
    concatenate x4 -> x0, local copies, waits for them, and re-layouts: 4.08 us -> none  [per_device(): windows = jnp.concatenate([blocks[:-1], blocks[1:]], 1)]
    ppermute x2 -> x0, starting transfers between devices: 3.54 us -> none  [passed_along(): lax.ppermute(value, axis, [(source, source + steps) for source in range(f...]
    slice x6 -> x0, local copies, waits for them, and re-layouts: 3.05 us -> none  [the longest x2 2.07 us: per_device(): windows = jnp.concatenate([blocks[:-1], blocks[1:]], 1)]
  transfers between devices with their start and end apart: 3 -> 0, of which waited for: 2 -> 0; matrix products, arithmetic and copies ran while one was open for 4% -> 0% of each run, Pallas kernels for 0% -> 0%
where the time goes in v2:
time: 148 us; the launch traced here: 147 us
  Pallas kernels  145 us (98%)
  local copies, waits for them, and re-layouts  1.87 us (1%)
    pallas_call x1, Pallas kernels, block_call(): pl.pallas_call(block_kernel, out_shape=jax.ShapeDtypeStruct((ROWS, WIDE),...  145 us

profile of v2, /device:TPU:1, one launch (start us, length us, event | category | flops | bytes accessed | tf_op | source)
XLA Modules:
  0.0 147.4 jit_solution(6797212530296380731)
XLA Ops:
  0.0 145.5 %block.1 = bf16[512,512]{1,0:T(8,128)(2,1)} custom-call(bf16[512,512]{1,0:T(8,128)(2,1)} %x_hbm.1, f32[16,1,512]{2,1,0:T(1,128)} %bitcast.5, bf16[3,512,256]{2,1,0:T(8,128)(2,1)} %bitcast.4, f32[3,3,256]{2,1,0:T(4,128)} %short_ref.1, f32[16,128]{1,0:T(8,128)} %bitcast.6, f32[1,256]{1,0:T(1,128)} %bitcast.7, bf16[256,8192]{1,0:T(8,128)(2,1)} %wo_hbm.1), custom_call_target="tpu_custom_call" | custom-call | tf_op jit(solution)/shard_map/block/pallas_call | solution.py:473
  145.5 1.9 %copy.9 = bf16[512,512]{1,0:T(8,128)(2,1)} copy(bf16[512,512]{1,0:T(8,128)(2,1)} %block.1) | data formatting | bytes 1048576

commit v3 on v2

v3 whole, which is shorter than its diff:
```python
import jax
import jax.numpy as jnp
from jax import lax
from jax.experimental import pallas as pl
from jax.experimental.pallas import tpu as pltpu
from jax.sharding import PartitionSpec as P

TAPS = 128
GROUP = 16
EPSILON = 1e-06
MESH = pl.DeviceIdType.MESH
ROWS = 512
WIDE = 512
CH = 256
F32 = jnp.float32
BF16 = jnp.bfloat16
PIECES = 4
PIECE = ROWS // PIECES
CUTS = (0, 112, 240, 368, 512)


def block_kernel(
    x_hbm, gain_ref, w_hbm, short_ref, taps_ref, skip_ref, wo_hbm, out_ref,
    tok, tg, wkv, wq, acc, cs, cr, sq, ss, sr, wo, toep, pj, pe, mix, gate, sb, rb, yb, yr, xres,
    loc, w_send, w_recv, y_send, y_recv, x_send, x_recv, d_send, d_recv, c_send, c_recv, s_send, s_recv,
    o_loc, o_send, o_recv, h_send, h_recv, g_send, g_recv, r_send, r_recv, v_send, v_recv,
):
    s = lax.axis_index("seq")
    c = lax.axis_index("chan")
    y_lo, z = s // 8, s % 8
    y_hi, x, core = c // 8, (c // 2) % 4, c % 2
    f_own = x * 2 + core
    x_right, x_left, x_far = (x + 1) % 4, (x + 3) % 4, (x + 2) % 4
    other = 1 - y_lo

    def at(y_hi_=y_hi, x_=x, core_=core, y_lo_=y_lo, z_=z):
        return (y_lo_ * 8 + z_, y_hi_ * 8 + x_ * 2 + core_)

    right, left = at(x_=x_right), at(x_=x_left)
    up, down = at(z_=(z + 1) % 8), at(z_=(z + 7) % 8)
    twin = at(core_=1 - core)
    mate = at(y_lo_=other)
    opposite = at(y_hi_=1 - y_hi)
    diagonal = at(y_hi_=1 - y_hi, y_lo_=other)
    after, before = ((s + 1) % 16, c), ((s + 15) % 16, c)

    def remote(src, dst, send, recv, device):
        return pltpu.make_async_remote_copy(
            src_ref=src, dst_ref=dst, send_sem=send, recv_sem=recv, device_id=device, device_id_type=MESH
        )

    own_w = []
    for h in range(2):
        rows = pl.ds(h * 256, 256)
        own_w.append(pltpu.make_async_copy(w_hbm.at[pl.ds(1, 2), rows, :], wkv.at[z, h], loc.at[h]))
    for h in range(2):
        rows = pl.ds(h * 256, 256)
        own_w.append(pltpu.make_async_copy(w_hbm.at[0, rows, :], wq.at[z, h], loc.at[2 + h]))
    for cp in own_w:
        cp.start()

    barrier = pltpu.get_barrier_semaphore()
    peers = (right, left, up, down, twin, mate, opposite, diagonal, after, before)
    for peer in peers:
        pl.semaphore_signal(barrier, inc=1, device_id=peer, device_id_type=MESH)
    pl.semaphore_wait(barrier, len(peers))

    def w_slot(phase, direction, distance, half):
        source = (z + 8 - distance) % 8 if direction == 0 else (z + distance) % 8
        return (wkv, wq)[phase].at[source, half]

    def recv_place(direction, k):
        if k == 6:
            return 4, direction
        return k // 2 + 1, k % 2

    def send_place(direction, k):
        if k < 2:
            return 0, k
        if k == 6:
            return 3, direction
        return (k - 2) // 2 + 1, (k - 2) % 2

    def w_copy(phase, direction, k):
        slot = w_slot(phase, direction, *send_place(direction, k))
        return remote(
            slot, slot, w_send.at[phase, direction, k], w_recv.at[phase, direction, k], up if direction == 0 else down
        )

    def w_wait(phase, direction, k):
        slot = w_slot(phase, direction, *recv_place(direction, k))
        remote(slot, slot, w_send.at[phase, direction, k], w_recv.at[phase, direction, k], up).wait_recv()

    def w_step(phase, k):
        for direction in range(2):
            w_wait(phase, direction, k - 2)
            if k < 6:
                w_copy(phase, direction, k).start()
            elif k - 6 == direction:
                w_copy(phase, direction, 6).start()

    for h in range(2):
        own_w[h].wait()
        for direction in range(2):
            w_copy(0, direction, h).start()

    is_home = y_hi == y_lo

    def piece(q):
        return pl.ds(q * PIECE, PIECE)

    def y_copy(d, q):
        return remote(
            x_hbm.at[piece(q), :], tok.at[y_lo, f_own, piece(q), :],
            y_send.at[d, q], y_recv.at[y_lo, q], at(y_lo_=y_hi, y_hi_=d),
        )

    def y_keep(q):
        return pltpu.make_async_copy(x_hbm.at[piece(q), :], tok.at[y_lo, f_own, piece(q), :], loc.at[5 + q])

    for q in range(PIECES):
        for d in range(2):
            stays = jnp.logical_and(is_home, y_hi == d)

            @pl.when(jnp.logical_not(stays))
            def _():
                y_copy(d, q).start()

            @pl.when(stays)
            def _():
                y_keep(q).start()

    def columns(d, core_):
        return wo_hbm.at[:, pl.ds(pl.multiple_of((d * 2 + core_) * WIDE, WIDE), WIDE)]

    def o_keep(d):
        return pltpu.make_async_copy(columns(d, core), wo.at[core, d], o_loc.at[d])

    def o_copy(d):
        return remote(columns(d, 1 - core), wo.at[core, d], o_send.at[d], o_recv.at[d], twin)

    for d in range(8):
        o_copy(d).start()
        o_keep(d).start()
    keep_x = pltpu.make_async_copy(x_hbm, xres, loc.at[4])
    keep_x.start()

    def x_place(direction, k):
        u = direction if k != 1 else 1 - direction
        return u, (x_far if k == 2 else x_left if direction == 0 else x_right)

    def x_copy(direction, k, q):
        if k < 2:
            slot = tok.at[direction if k == 0 else 1 - direction, f_own, piece(q), :]
        else:
            slot = tok.at[direction, (x_left if direction == 0 else x_right) * 2 + core, piece(q), :]
        return remote(
            slot, slot, x_send.at[direction, k, q], x_recv.at[direction, k, q], right if direction == 0 else left
        )

    def x_wait(direction, k, q):
        u, source = x_place(direction, k)
        slot = tok.at[u, source * 2 + core, piece(q), :]
        remote(slot, slot, x_send.at[direction, k, q], x_recv.at[direction, k, q], right).wait_recv()

    places = [(0, x), (1, x)] + [x_place(direction, k) for k in range(3) for direction in range(2)]

    def d_copy(index, q, core_):
        u, source = places[index]
        slot = tok.at[u, source * 2 + core_, piece(q), :]
        return remote(slot, slot, d_send.at[index, q], d_recv.at[index, q], twin)

    def y_arrived(q):
        for u in range(2):
            stays = jnp.logical_and(is_home, y_lo == u)
            slot = tok.at[u, f_own, piece(q), :]

            @pl.when(jnp.logical_not(stays))
            def _():
                remote(slot, slot, y_send.at[0, q], y_recv.at[u, q], right).wait_recv()

            @pl.when(stays)
            def _():
                y_keep(q).wait()

        for k in range(2):
            for direction in range(2):
                x_copy(direction, k, q).start()
        for index in range(2):
            d_copy(index, q, core).start()

    def x_arrived(k, q):
        for direction in range(2):
            x_wait(direction, k, q)
            if k == 0:
                x_copy(direction, 2, q).start()
            d_copy(2 + 2 * k + direction, q, core).start()

    def scaled(index, q, core_):
        u, source = places[index]
        f = source * 2 + core_

        def body(i, carry):
            rows = pl.ds(pl.multiple_of(q * PIECE + i * 64, 64), 64)
            raw = tok[u, f, rows, :].astype(F32)
            gain = gain_ref[pl.ds(y_lo * 8 + f, 1), 0, :]
            tg[u, f, rows, :] = (raw * gain).astype(BF16)
            square = raw * raw
            sq[u, rows, :] += square[:, 0:128] + square[:, 128:256] + square[:, 256:384] + square[:, 384:512]
            return carry

        lax.fori_loop(0, PIECE // 64, body, 0)

    def taken(indices, pieces):
        for index in indices:
            for q in pieces:
                scaled(index, q, core)
                d_copy(index, q, 1 - core).wait_recv()
                scaled(index, q, 1 - core)

    acc[...] = jnp.zeros_like(acc)
    sq[...] = jnp.zeros_like(sq)
    y_arrived(0)
    w_step(0, 2)
    y_arrived(1)
    w_step(0, 3)
    y_arrived(2)
    y_arrived(3)
    x_arrived(0, 0)
    w_step(0, 4)
    x_arrived(0, 1)

    spread = (
        lax.broadcasted_iota(jnp.int32, (TAPS, 2 * TAPS), 0) + lax.broadcasted_iota(jnp.int32, (TAPS, 2 * TAPS), 1)
        == TAPS
    ).astype(F32)
    first = jnp.dot(taps_ref[...], spread, precision=lax.Precision.HIGHEST, preferred_element_type=F32)
    for g in range(16):
        row = jnp.broadcast_to(first[g : g + 1, :], (TAPS, 2 * TAPS))
        matrix = pltpu.roll(row, 0, 1, stride=1, stride_axis=0)
        high = matrix.astype(BF16)
        toep[0, g] = high
        toep[1, g] = (matrix - high.astype(F32)).astype(BF16)

    w_step(0, 5)
    x_arrived(0, 2)
    taken((0, 1), (0, 1))
    w_step(0, 6)
    x_arrived(0, 3)
    taken((0, 1), (2, 3))
    w_step(0, 7)
    for h in range(2):
        own_w[2 + h].wait()
        for direction in range(2):
            w_copy(1, direction, h).start()
    for q in range(PIECES):
        x_arrived(1, q)
        taken((2, 3), (q,))
    for q in range(PIECES):
        taken((4, 5), (q,))
    for q in range(PIECES):
        x_arrived(2, q)
        taken((6, 7), (q,))

    def row_sums(u):
        column = jnp.sum(sq[u], axis=1, keepdims=True)
        return jnp.transpose(jnp.broadcast_to(column, (ROWS, 128)))[0:8, :]

    ss[...] = row_sums(other)
    s_copy = remote(ss, sr, s_send, s_recv, mate)
    s_copy.start()

    def add_kv(u, low, count):
        rows = pl.ds(low, count)

        def body(f, carry):
            lhs0, lhs1 = tg[u, f, rows, 0:256], tg[u, f, rows, 256:512]
            for p in range(2):
                part = jnp.dot(lhs0, wkv[f, 0, p], preferred_element_type=F32)
                part += jnp.dot(lhs1, wkv[f, 1, p], preferred_element_type=F32)
                acc[u, 1 + p, rows, :] += part
            return carry

        lax.fori_loop(0, 8, body, 0)

    def add_q(u, f, low, count):
        rows = pl.ds(low, count)
        part = jnp.dot(tg[u, f, rows, 0:256], wq[f, 0], preferred_element_type=F32)
        part += jnp.dot(tg[u, f, rows, 256:512], wq[f, 1], preferred_element_type=F32)
        return acc[u, 0, rows, :] + part

    def add_q_chunk(f):
        for u in range(2):
            for low in (0, 256):
                acc[u, 0, pl.ds(low, 256), :] = add_q(u, f, low, 256)

    kv_cuts = ((240, 272), (0, 240))

    def c_kv(i):
        rows = pl.ds(*kv_cuts[i])
        planes = pl.ds(1, 2)
        return remote(cs.at[planes, rows, :], cr.at[planes, rows, :], c_send.at[i], c_recv.at[i], mate)

    def c_q(r):
        rows = pl.ds(CUTS[r], CUTS[r + 1] - CUTS[r])
        return remote(cs.at[0, rows, :], cr.at[0, rows, :], c_send.at[2 + r], c_recv.at[2 + r], mate)

    def give_kv(i):
        add_kv(other, *kv_cuts[i])
        rows = pl.ds(*kv_cuts[i])
        for p in (1, 2):
            cs[p, rows, :] = acc[other, p, rows, :].astype(BF16)
        c_kv(i).start()

    def finish(p, low, count):
        rows = pl.ds(low, count)
        factor = sq[0, rows, :]
        factor = jnp.concatenate([factor, factor], axis=1)
        value = acc[y_lo, p, rows, :] + cr[p, rows, :].astype(F32)
        pj[p, pl.ds(16 + low, count), :] = (value * factor).astype(BF16)

    def filtered(p, r):
        extended = pj[p, pl.ds(r * 128, 144), :].astype(F32)
        taps = [short_ref[k, pl.ds(p, 1), :] for k in range(3)]
        return taps[0] * extended[16:144] + taps[1] * extended[15:143] + taps[2] * extended[14:142]

    def make_product(r):
        pe[pl.ds(128 + r * 128, 128), :] = (filtered(1, r) * filtered(2, r)).astype(BF16)

    kv_planes = pl.ds(1, 2)
    halo_kv = [
        remote(pe.at[pl.ds(512, 128), :], pe.at[pl.ds(0, 128), :], h_send.at[0], h_recv.at[0], after),
        remote(pj.at[kv_planes, pl.ds(512, 16), :], pj.at[kv_planes, pl.ds(0, 16), :], h_send.at[1], h_recv.at[1], after),
    ]
    halo_q = remote(pj.at[0, pl.ds(512, 16), :], pj.at[0, pl.ds(0, 16), :], h_send.at[2], h_recv.at[2], after)
    has_after, has_before = s < 15, s > 0

    group_of_lane = lax.broadcasted_iota(jnp.int32, (128, CH), 1) // GROUP

    def make_mixing(r):
        window = pe[pl.ds(r * 128, 256), :]

        def body(g, mixed):
            part = jnp.dot(toep[0, g], window, preferred_element_type=F32)
            part += jnp.dot(toep[1, g], window, preferred_element_type=F32)
            return jnp.where(group_of_lane == g, part, mixed)

        mixed = lax.fori_loop(0, 16, body, jnp.zeros((128, CH), F32), unroll=4)
        product = pe[pl.ds(128 + r * 128, 128), :].astype(F32)
        mix[pl.ds(r * 128, 128), :] = skip_ref[...] * product + mixed

    for direction in range(2):
        w_wait(0, direction, 6)
    give_kv(0)
    w_step(1, 2)
    give_kv(1)
    w_step(1, 3)
    add_kv(y_lo, 240, 272)
    w_step(1, 4)
    add_kv(y_lo, 0, 240)
    s_copy.wait()
    total = row_sums(y_lo) + sr[...]
    factor = lax.rsqrt(total * (1.0 / 8192.0) + EPSILON)
    sq[0] = jnp.transpose(jnp.broadcast_to(factor[0:1, :], (128, ROWS)))

    @pl.when(s == 0)
    def _():
        pe[pl.ds(0, 128), :] = jnp.zeros((128, CH), BF16)
        pj[:, pl.ds(0, 16), :] = jnp.zeros((3, 16, CH), BF16)

    w_step(1, 5)
    c_kv(0).wait_recv()
    for p in (1, 2):
        finish(p, *kv_cuts[0])
    make_product(3)

    @pl.when(has_after)
    def _():
        for cp in halo_kv:
            cp.start()

    make_product(2)
    w_step(1, 6)
    make_mixing(3)
    for distance in (0, 1, 2):
        add_q_chunk((z + distance) % 8)
        if distance:
            add_q_chunk((z + 8 - distance) % 8)
    w_step(1, 7)
    c_kv(1).wait_recv()
    for p in (1, 2):
        finish(p, *kv_cuts[1])
    make_product(1)
    make_mixing(2)
    add_q_chunk((z + 3) % 8)
    add_q_chunk((z + 5) % 8)

    @pl.when(has_before)
    def _():
        for cp in halo_kv:
            cp.wait_recv()

    make_product(0)
    make_mixing(1)
    make_mixing(0)
    for d in range(8):
        o_keep(d).wait()
        remote(wo.at[1 - core, d], wo.at[1 - core, d], o_send.at[d], o_recv.at[d], twin).wait_recv()
    keep_x.wait()

    for direction in range(2):
        w_wait(1, direction, 6)
    f_last = (z + 4) % 8
    for r in (3, 2, 1, 0):
        low, count = CUTS[r], CUTS[r + 1] - CUTS[r]
        cs[0, pl.ds(low, count), :] = add_q(other, f_last, low, count).astype(BF16)
        c_q(r).start()
    for low in (256, 0):
        acc[y_lo, 0, pl.ds(low, 256), :] = add_q(y_lo, f_last, low, 256)

    def g_copy(r):
        place = gate.at[core, pl.ds(r * 128, 128), :]
        return remote(place, place, g_send.at[r], g_recv.at[r], twin)

    def make_gating(r):
        rows = pl.ds(r * 128, 128)
        gate[core, rows, :] = (filtered(0, r) * mix[rows, :]).astype(BF16)
        g_copy(r).start()

    def arrive_q(r):
        c_q(r).wait_recv()
        finish(0, CUTS[r], CUTS[r + 1] - CUTS[r])

    def block(r, x_, y_hi_):
        d = y_hi_ * 4 + x_
        rows = pl.ds(r * 128, 128)
        part = jnp.dot(gate[0, rows, :], wo[0, d], preferred_element_type=F32)
        return part + jnp.dot(gate[1, rows, :], wo[1, d], preferred_element_type=F32)

    def r_copy(r, direction, k):
        return remote(
            sb.at[r, direction, k], rb.at[r, direction, k], r_send.at[r, direction, k], r_recv.at[r, direction, k],
            right if direction == 0 else left,
        )

    def v_copy(r):
        return remote(yb.at[r], yr.at[r], v_send.at[r], v_recv.at[r], opposite)

    nears = (x_right, x_left)

    def send_first(r):
        twin_place = gate.at[1 - core, pl.ds(r * 128, 128), :]
        remote(twin_place, twin_place, g_send.at[r], g_recv.at[r], twin).wait_recv()
        for direction in range(2):
            sb[r, direction, 0] = block(r, x_far, direction).astype(BF16)
            r_copy(r, direction, 0).start()
        for direction in range(2):
            sb[r, direction, 1] = block(r, nears[direction], 1 - direction).astype(BF16)
            r_copy(r, direction, 1).start()

    def send_joined(r):
        for direction in range(2):
            mine = block(r, nears[direction], direction)
            r_copy(r, direction, 0).wait_recv()
            sb[r, direction, 2] = (mine + rb[r, direction, 0].astype(F32)).astype(BF16)
            r_copy(r, direction, 2).start()

    def summed(r, y_hi_):
        mine = block(r, x, y_hi_)
        alone, joined = rb[r, 1 - y_hi_, 1], rb[r, y_hi_, 2]
        return mine + alone.astype(F32) + joined.astype(F32)

    def send_across(r):
        for direction in range(2):
            r_copy(r, direction, 1).wait_recv()
            r_copy(r, direction, 2).wait_recv()
        yb[r] = summed(r, 1 - y_hi).astype(BF16)
        v_copy(r).start()

    def write(r):
        rows = pl.ds(r * 128, 128)
        mine = summed(r, y_hi) + xres[rows, :].astype(F32)
        v_copy(r).wait_recv()
        out_ref[rows, :] = (mine + yr[r].astype(F32)).astype(BF16)

    arrive_q(3)

    @pl.when(has_after)
    def _():
        halo_q.start()

    make_gating(3)
    arrive_q(2)
    make_gating(2)
    send_first(3)
    arrive_q(1)
    make_gating(1)
    send_first(2)
    arrive_q(0)

    @pl.when(has_before)
    def _():
        halo_q.wait_recv()

    make_gating(0)
    send_joined(3)
    send_first(1)
    send_joined(2)
    send_first(0)
    send_across(3)
    send_joined(1)
    send_across(2)
    write(3)
    send_joined(0)
    send_across(1)
    write(2)
    send_across(0)
    write(1)
    write(0)

    for direction in range(2):
        for k in range(7):
            for phase in range(2):
                w_copy(phase, direction, k).wait_send()
        for k in range(3):
            for q in range(PIECES):
                x_copy(direction, k, q).wait_send()
    for d in range(2):

        @pl.when(jnp.logical_not(jnp.logical_and(is_home, y_hi == d)))
        def _():
            for q in range(PIECES):
                y_copy(d, q).wait_send()

    for index in range(8):
        for q in range(PIECES):
            d_copy(index, q, core).wait_send()
    for i in range(2):
        c_kv(i).wait_send()
    for d in range(8):
        o_copy(d).wait_send()
    for r in range(4):
        c_q(r).wait_send()
        g_copy(r).wait_send()
        v_copy(r).wait_send()
        for direction in range(2):
            for k in range(3):
                r_copy(r, direction, k).wait_send()

    @pl.when(has_after)
    def _():
        for cp in halo_kv + [halo_q]:
            cp.wait_send()


def block_call(tokens, gain, w_planes, short_taps, taps, skip, w_out):
    dma = pltpu.SemaphoreType.DMA
    vmem = pl.BlockSpec(memory_space=pltpu.VMEM)
    far = pl.BlockSpec(memory_space=pl.ANY)
    return pl.pallas_call(
        block_kernel,
        out_shape=jax.ShapeDtypeStruct((ROWS, WIDE), BF16),
        in_specs=[far, vmem, far, vmem, vmem, vmem, far],
        out_specs=vmem,
        scratch_shapes=[
            pltpu.VMEM((2, 8, ROWS, WIDE), BF16),
            pltpu.VMEM((2, 8, ROWS, WIDE), BF16),
            pltpu.VMEM((8, 2, 2, 256, CH), BF16),
            pltpu.VMEM((8, 2, 256, CH), BF16),
            pltpu.VMEM((2, 3, ROWS, CH), F32),
            pltpu.VMEM((3, ROWS, CH), BF16),
            pltpu.VMEM((3, ROWS, CH), BF16),
            pltpu.VMEM((2, ROWS, 128), F32),
            pltpu.VMEM((8, ROWS), F32),
            pltpu.VMEM((8, ROWS), F32),
            pltpu.VMEM((2, 8, CH, WIDE), BF16),
            pltpu.VMEM((2, 16, TAPS, 2 * TAPS), BF16),
            pltpu.VMEM((3, 16 + ROWS, CH), BF16),
            pltpu.VMEM((128 + ROWS, CH), BF16),
            pltpu.VMEM((ROWS, CH), F32),
            pltpu.VMEM((2, ROWS, CH), BF16),
            pltpu.VMEM((4, 2, 3, 128, WIDE), BF16),
            pltpu.VMEM((4, 2, 3, 128, WIDE), BF16),
            pltpu.VMEM((4, 128, WIDE), BF16),
            pltpu.VMEM((4, 128, WIDE), BF16),
            pltpu.VMEM((ROWS, WIDE), BF16),
            dma((9,)),
            dma((2, 2, 7)), dma((2, 2, 7)),
            dma((2, PIECES)), dma((2, PIECES)),
            dma((2, 3, PIECES)), dma((2, 3, PIECES)),
            dma((8, PIECES)), dma((8, PIECES)),
            dma((6,)), dma((6,)),
            dma, dma,
            dma((8,)), dma((8,)), dma((8,)),
            dma((3,)), dma((3,)),
            dma((4,)), dma((4,)),
            dma((4, 2, 3)), dma((4, 2, 3)),
            dma((4,)), dma((4,)),
        ],
        compiler_params=pltpu.CompilerParams(
            collective_id=0, has_side_effects=True, vmem_limit_bytes=58 * 1024 * 1024
        ),
        name="block",
    )(tokens, gain, w_planes, short_taps, taps, skip, w_out)


def per_device(tokens, norm_gain, w_in, short_taps, medium_taps, skip_gain, w_out):
    return block_call(
        tokens,
        norm_gain.reshape(16, 1, WIDE),
        jnp.transpose(w_in, (1, 0, 2)),
        short_taps,
        jnp.transpose(medium_taps),
        skip_gain.reshape(1, CH),
        w_out,
    )


def solution(mesh):
    in_specs = (
        P("seq", "chan"),
        P(),
        P("seq", None, "chan"),
        P(None, None, "chan"),
        P(None, "chan"),
        P("chan"),
        P("chan", None),
    )
    out_specs = P("seq", "chan")
    return jax.shard_map(
        per_device, mesh=mesh, in_specs=in_specs, out_specs=out_specs, check_vma=False
    )
```

time: 148 us -> 137 us (0.926)
  Pallas kernels: 145 us -> 135 us
    pallas_call x1, Pallas kernels: 145 us -> 135 us  [block_call(): pl.pallas_call(block_kernel, out_shape=jax.ShapeDtypeStruct((ROWS, WIDE),...]
where the time goes in v3:
time: 137 us
  Pallas kernels  135 us (99%)
  local copies, waits for them, and re-layouts  1.87 us (1%)
    pallas_call x1, Pallas kernels, block_call(): pl.pallas_call(block_kernel, out_shape=jax.ShapeDtypeStruct((ROWS, WIDE),...  135 us

profile of v3, /device:TPU:1, one launch (start us, length us, event | category | flops | bytes accessed | tf_op | source)
XLA Modules:
  0.0 136.9 jit_solution(7486463647754574944)
XLA Ops:
  0.0 135.0 %block.1 = bf16[512,512]{1,0:T(8,128)(2,1)} custom-call(bf16[512,512]{1,0:T(8,128)(2,1)} %x_hbm.1, f32[16,1,512]{2,1,0:T(1,128)} %bitcast.5, bf16[3,512,256]{2,1,0:T(8,128)(2,1)} %bitcast.4, f32[3,3,256]{2,1,0:T(4,128)} %short_ref.1, f32[16,128]{1,0:T(8,128)} %bitcast.6, f32[1,256]{1,0:T(1,128)} %bitcast.7, bf16[256,8192]{1,0:T(8,128)(2,1)} %wo_hbm.1), custom_call_target="tpu_custom_call" | custom-call | tf_op jit(solution)/shard_map/block/pallas_call | solution.py:560
  135.0 1.9 %copy.9 = bf16[512,512]{1,0:T(8,128)(2,1)} copy(bf16[512,512]{1,0:T(8,128)(2,1)} %block.1) | data formatting | bytes 1048576

commit v4 on v3

--- a/solution.py
+++ b/solution.py
@@ -16,14 +16,16 @@
 BF16 = jnp.bfloat16
 PIECES = 4
 PIECE = ROWS // PIECES
-CUTS = (0, 112, 240, 368, 512)
+CHUNKS = 2
+CHUNK = ROWS // CHUNKS
+CUTS = [0] + [r * CHUNK - 16 for r in range(1, CHUNKS)] + [ROWS]
 
 
 def block_kernel(
     x_hbm, gain_ref, w_hbm, short_ref, taps_ref, skip_ref, wo_hbm, out_ref,
-    tok, tg, wkv, wq, acc, cs, cr, sq, ss, sr, wo, toep, pj, pe, mix, gate, sb, rb, yb, yr, xres,
-    loc, w_send, w_recv, y_send, y_recv, x_send, x_recv, d_send, d_recv, c_send, c_recv, s_send, s_recv,
-    o_loc, o_send, o_recv, h_send, h_recv, g_send, g_recv, r_send, r_recv, v_send, v_recv,
+    tok, tg, wkv, wq, stage, acc, cs, cr, sq, ss, sr, wo, toep, pj, pe, mix, gate, xres,
+    loc, w_send, w_recv, y_send, y_recv, f_send, f_recv, x_send, x_recv, d_send, d_recv, c_send, c_recv, s_send, s_recv,
+    o_send, o_recv, m_send, m_recv, h_send, h_recv, v_send, v_recv, a_send, a_recv, t_send, t_recv,
 ):
     s = lax.axis_index("seq")
     c = lax.axis_index("chan")
@@ -60,7 +62,17 @@
         cp.start()
 
     barrier = pltpu.get_barrier_semaphore()
-    peers = (right, left, up, down, twin, mate, opposite, diagonal, after, before)
+    def w_out_peers(y_hi_, y_lo_, xs):
+        return [at(y_hi_=y_hi_, y_lo_=y_lo_, x_=x_, core_=k) for x_ in xs for k in range(2)]
+
+    o_peers = (
+        w_out_peers(y_hi, y_lo, (x_right, x_left))
+        + w_out_peers(1 - y_hi, other, (x_right, x_left))
+        + w_out_peers(y_hi, y_lo, (x_far,))
+        + w_out_peers(1 - y_hi, other, (x_far, x))
+        + [twin]
+    )
+    peers = o_peers + [up, down, mate, opposite, after, before]
     for peer in peers:
         pl.semaphore_signal(barrier, inc=1, device_id=peer, device_id_type=MESH)
     pl.semaphore_wait(barrier, len(peers))
@@ -118,30 +130,59 @@
     def y_keep(q):
         return pltpu.make_async_copy(x_hbm.at[piece(q), :], tok.at[y_lo, f_own, piece(q), :], loc.at[5 + q])
 
+    SHARED = (8, 9, 10, 11)
+    odd = z % 2
+    buddy = at(z_=z + 1 - 2 * odd)
+
+    def o_rows(i, half):
+        return pl.ds(pl.multiple_of(half * 128, 128), 128) if i in SHARED else pl.ds(0, 256)
+
+    def o_copy(i):
+        device = o_peers[i]
+        rows = o_rows(i, odd)
+        there = wo_hbm.at[rows, pl.ds(pl.multiple_of(device[1] * WIDE, WIDE), WIDE)]
+        return remote(there, wo.at[c, rows, :], o_send.at[i], o_recv.at[c], device)
+
+    def o_wait(i):
+        source = o_peers[i][1]
+        slot = wo.at[source, o_rows(i, odd), :]
+        remote(slot, slot, o_send.at[i], o_recv.at[source], twin).wait_recv()
+
+    def m_copy(i):
+        slot = wo.at[o_peers[i][1], o_rows(i, odd), :]
+        return remote(slot, slot, m_send.at[i], m_recv.at[i], buddy)
+
+    def m_wait(i):
+        slot = wo.at[o_peers[i][1], o_rows(i, 1 - odd), :]
+        remote(slot, slot, m_send.at[i], m_recv.at[i], buddy).wait_recv()
+
+    o_keep = pltpu.make_async_copy(wo_hbm.at[:, pl.ds(pl.multiple_of(c * WIDE, WIDE), WIDE)], wo.at[c], loc.at[9])
+
+    def f_copy(q):
+        return remote(x_hbm.at[piece(q), :], stage.at[piece(q), :], f_send.at[q], f_recv.at[q], diagonal)
+
+    def f_pass(q):
+        return remote(
+            stage.at[piece(q), :], tok.at[other, f_own, piece(q), :], y_send.at[1 - y_hi, q], y_recv.at[other, q], mate
+        )
+
     for q in range(PIECES):
         for d in range(2):
             stays = jnp.logical_and(is_home, y_hi == d)
 
-            @pl.when(jnp.logical_not(stays))
+            @pl.when(jnp.logical_not(is_home))
             def _():
                 y_copy(d, q).start()
 
             @pl.when(stays)
             def _():
                 y_keep(q).start()
-
-    def columns(d, core_):
-        return wo_hbm.at[:, pl.ds(pl.multiple_of((d * 2 + core_) * WIDE, WIDE), WIDE)]
-
-    def o_keep(d):
-        return pltpu.make_async_copy(columns(d, core), wo.at[core, d], o_loc.at[d])
-
-    def o_copy(d):
-        return remote(columns(d, 1 - core), wo.at[core, d], o_send.at[d], o_recv.at[d], twin)
-
-    for d in range(8):
-        o_copy(d).start()
-        o_keep(d).start()
+                f_copy(q).start()
+
+    for i in (8, 9, 10, 11):
+        o_copy(i).start()
+    o_copy(14).start()
+    o_keep.start()
     keep_x = pltpu.make_async_copy(x_hbm, xres, loc.at[4])
     keep_x.start()
 
@@ -170,24 +211,35 @@
         slot = tok.at[u, source * 2 + core_, piece(q), :]
         return remote(slot, slot, d_send.at[index, q], d_recv.at[index, q], twin)
 
+    def send_own(u, q):
+        for direction in range(2):
+            k = 1 - u if direction else u
+            slot = tok.at[u, f_own, piece(q), :]
+            remote(
+                slot, slot, x_send.at[direction, k, q], x_recv.at[direction, k, q], right if direction == 0 else left
+            ).start()
+        slot = tok.at[u, f_own, piece(q), :]
+        remote(slot, slot, d_send.at[u, q], d_recv.at[u, q], twin).start()
+
     def y_arrived(q):
-        for u in range(2):
-            stays = jnp.logical_and(is_home, y_lo == u)
-            slot = tok.at[u, f_own, piece(q), :]
-
-            @pl.when(jnp.logical_not(stays))
-            def _():
-                remote(slot, slot, y_send.at[0, q], y_recv.at[u, q], right).wait_recv()
-
-            @pl.when(stays)
-            def _():
-                y_keep(q).wait()
-
-        for k in range(2):
-            for direction in range(2):
-                x_copy(direction, k, q).start()
-        for index in range(2):
-            d_copy(index, q, core).start()
+        slot = tok.at[other, f_own, piece(q), :]
+        remote(slot, slot, y_send.at[0, q], y_recv.at[other, q], right).wait_recv()
+        send_own(other, q)
+
+    def y_far_arrived(q):
+        slot = tok.at[y_lo, f_own, piece(q), :]
+
+        @pl.when(is_home)
+        def _():
+            remote(stage.at[piece(q), :], stage.at[piece(q), :], f_send.at[q], f_recv.at[q], right).wait_recv()
+            f_pass(q).start()
+            y_keep(q).wait()
+
+        @pl.when(jnp.logical_not(is_home))
+        def _():
+            remote(slot, slot, y_send.at[0, q], y_recv.at[y_lo, q], right).wait_recv()
+
+        send_own(y_lo, q)
 
     def x_arrived(k, q):
         for direction in range(2):
@@ -222,10 +274,14 @@
     sq[...] = jnp.zeros_like(sq)
     y_arrived(0)
     w_step(0, 2)
+    y_far_arrived(0)
     y_arrived(1)
+    y_far_arrived(1)
     w_step(0, 3)
     y_arrived(2)
+    y_far_arrived(2)
     y_arrived(3)
+    y_far_arrived(3)
     x_arrived(0, 0)
     w_step(0, 4)
     x_arrived(0, 1)
@@ -244,10 +300,12 @@
 
     w_step(0, 5)
     x_arrived(0, 2)
-    taken((0, 1), (0, 1))
+    taken((0, 1), range(PIECES // 2))
     w_step(0, 6)
     x_arrived(0, 3)
-    taken((0, 1), (2, 3))
+    for i in (0, 2, 1, 3, 4, 6, 5, 7, 12, 13):
+        o_copy(i).start()
+    taken((0, 1), range(PIECES // 2, PIECES))
     w_step(0, 7)
     for h in range(2):
         own_w[2 + h].wait()
@@ -256,11 +314,15 @@
     for q in range(PIECES):
         x_arrived(1, q)
         taken((2, 3), (q,))
-    for q in range(PIECES):
-        taken((4, 5), (q,))
-    for q in range(PIECES):
-        x_arrived(2, q)
-        taken((6, 7), (q,))
+    taken((4, 5), range(PIECES))
+    w_step(1, 2)
+    x_arrived(2, 0)
+    x_arrived(2, 1)
+    taken((6, 7), (0, 1))
+    w_step(1, 3)
+    x_arrived(2, 2)
+    x_arrived(2, 3)
+    taken((6, 7), (2, 3))
 
     def row_sums(u):
         column = jnp.sum(sq[u], axis=1, keepdims=True)
@@ -319,13 +381,13 @@
         value = acc[y_lo, p, rows, :] + cr[p, rows, :].astype(F32)
         pj[p, pl.ds(16 + low, count), :] = (value * factor).astype(BF16)
 
-    def filtered(p, r):
-        extended = pj[p, pl.ds(r * 128, 144), :].astype(F32)
+    def filtered(p, low, n):
+        extended = pj[p, pl.ds(low, n + 16), :].astype(F32)
         taps = [short_ref[k, pl.ds(p, 1), :] for k in range(3)]
-        return taps[0] * extended[16:144] + taps[1] * extended[15:143] + taps[2] * extended[14:142]
+        return taps[0] * extended[16 : n + 16] + taps[1] * extended[15 : n + 15] + taps[2] * extended[14 : n + 14]
 
     def make_product(r):
-        pe[pl.ds(128 + r * 128, 128), :] = (filtered(1, r) * filtered(2, r)).astype(BF16)
+        pe[pl.ds(128 + r * 128, 128), :] = (filtered(1, r * 128, 128) * filtered(2, r * 128, 128)).astype(BF16)
 
     kv_planes = pl.ds(1, 2)
     halo_kv = [
@@ -352,12 +414,12 @@
     for direction in range(2):
         w_wait(0, direction, 6)
     give_kv(0)
-    w_step(1, 2)
+    w_step(1, 4)
     give_kv(1)
-    w_step(1, 3)
     add_kv(y_lo, 240, 272)
-    w_step(1, 4)
+    w_step(1, 5)
     add_kv(y_lo, 0, 240)
+    w_step(1, 6)
     s_copy.wait()
     total = row_sums(y_lo) + sr[...]
     factor = lax.rsqrt(total * (1.0 / 8192.0) + EPSILON)
@@ -368,7 +430,6 @@
         pe[pl.ds(0, 128), :] = jnp.zeros((128, CH), BF16)
         pj[:, pl.ds(0, 16), :] = jnp.zeros((3, 16, CH), BF16)
 
-    w_step(1, 5)
     c_kv(0).wait_recv()
     for p in (1, 2):
         finish(p, *kv_cuts[0])
@@ -380,13 +441,12 @@
             cp.start()
 
     make_product(2)
-    w_step(1, 6)
+    w_step(1, 7)
     make_mixing(3)
     for distance in (0, 1, 2):
         add_q_chunk((z + distance) % 8)
         if distance:
             add_q_chunk((z + 8 - distance) % 8)
-    w_step(1, 7)
     c_kv(1).wait_recv()
     for p in (1, 2):
         finish(p, *kv_cuts[1])
@@ -403,120 +463,119 @@
     make_product(0)
     make_mixing(1)
     make_mixing(0)
-    for d in range(8):
-        o_keep(d).wait()
-        remote(wo.at[1 - core, d], wo.at[1 - core, d], o_send.at[d], o_recv.at[d], twin).wait_recv()
+    o_keep.wait()
     keep_x.wait()
 
     for direction in range(2):
         w_wait(1, direction, 6)
     f_last = (z + 4) % 8
-    for r in (3, 2, 1, 0):
+    order = range(CHUNKS - 1, -1, -1)
+    for r in order:
         low, count = CUTS[r], CUTS[r + 1] - CUTS[r]
         cs[0, pl.ds(low, count), :] = add_q(other, f_last, low, count).astype(BF16)
         c_q(r).start()
+    for i in SHARED:
+        o_wait(i)
+        m_copy(i).start()
     for low in (256, 0):
         acc[y_lo, 0, pl.ds(low, 256), :] = add_q(y_lo, f_last, low, 256)
 
-    def g_copy(r):
-        place = gate.at[core, pl.ds(r * 128, 128), :]
-        return remote(place, place, g_send.at[r], g_recv.at[r], twin)
+    held = [(y_hi, x), (1 - y_hi, x)]
+    for y_hi_ in (y_hi, 1 - y_hi):
+        held += [(y_hi_, x_left), (y_hi_, x_right)]
+    held += [(y_hi, x_far), (1 - y_hi, x_far)]
+
+    def part_of(index, core_, r):
+        y_hi_, x_ = held[index]
+        return gate.at[y_hi_ * 8 + x_ * 2 + core_, pl.ds(r * CHUNK, CHUNK), :]
+
+    def t_copy(index, r):
+        place = part_of(index, core, r)
+        return remote(place, place, t_send.at[r, index], t_recv.at[r, index], twin)
+
+    def v_copy(r):
+        place = part_of(0, core, r)
+        return remote(place, place, v_send.at[r], v_recv.at[r], opposite)
+
+    def a_copy(direction, k, r):
+        index = k if k < 2 else 2 if direction == 0 else 5
+        place = part_of(index, core, r)
+        return remote(
+            place, place, a_send.at[r, direction, k], a_recv.at[r, direction, k], right if direction == 0 else left
+        )
+
+    def a_arrived(k, r):
+        for direction in range(2):
+            index = 2 + 2 * k + direction
+            place = part_of(index, core, r)
+            remote(place, place, a_send.at[r, direction, k], a_recv.at[r, direction, k], right).wait_recv()
+            if k == direction:
+                a_copy(direction, 2, r).start()
+            t_copy(index, r).start()
+
+    def v_arrived(r):
+        place = part_of(1, core, r)
+        remote(place, place, v_send.at[r], v_recv.at[r], opposite).wait_recv()
+        for direction in range(2):
+            a_copy(direction, 1, r).start()
+        t_copy(1, r).start()
 
     def make_gating(r):
-        rows = pl.ds(r * 128, 128)
-        gate[core, rows, :] = (filtered(0, r) * mix[rows, :]).astype(BF16)
-        g_copy(r).start()
+        rows = pl.ds(r * CHUNK, CHUNK)
+        gate[c, rows, :] = (filtered(0, r * CHUNK, CHUNK) * mix[rows, :]).astype(BF16)
+        v_copy(r).start()
+        for direction in range(2):
+            a_copy(direction, 0, r).start()
+        t_copy(0, r).start()
 
     def arrive_q(r):
         c_q(r).wait_recv()
         finish(0, CUTS[r], CUTS[r + 1] - CUTS[r])
 
-    def block(r, x_, y_hi_):
-        d = y_hi_ * 4 + x_
-        rows = pl.ds(r * 128, 128)
-        part = jnp.dot(gate[0, rows, :], wo[0, d], preferred_element_type=F32)
-        return part + jnp.dot(gate[1, rows, :], wo[1, d], preferred_element_type=F32)
-
-    def r_copy(r, direction, k):
-        return remote(
-            sb.at[r, direction, k], rb.at[r, direction, k], r_send.at[r, direction, k], r_recv.at[r, direction, k],
-            right if direction == 0 else left,
-        )
-
-    def v_copy(r):
-        return remote(yb.at[r], yr.at[r], v_send.at[r], v_recv.at[r], opposite)
-
-    nears = (x_right, x_left)
-
-    def send_first(r):
-        twin_place = gate.at[1 - core, pl.ds(r * 128, 128), :]
-        remote(twin_place, twin_place, g_send.at[r], g_recv.at[r], twin).wait_recv()
-        for direction in range(2):
-            sb[r, direction, 0] = block(r, x_far, direction).astype(BF16)
-            r_copy(r, direction, 0).start()
-        for direction in range(2):
-            sb[r, direction, 1] = block(r, nears[direction], 1 - direction).astype(BF16)
-            r_copy(r, direction, 1).start()
-
-    def send_joined(r):
-        for direction in range(2):
-            mine = block(r, nears[direction], direction)
-            r_copy(r, direction, 0).wait_recv()
-            sb[r, direction, 2] = (mine + rb[r, direction, 0].astype(F32)).astype(BF16)
-            r_copy(r, direction, 2).start()
-
-    def summed(r, y_hi_):
-        mine = block(r, x, y_hi_)
-        alone, joined = rb[r, 1 - y_hi_, 1], rb[r, y_hi_, 2]
-        return mine + alone.astype(F32) + joined.astype(F32)
-
-    def send_across(r):
-        for direction in range(2):
-            r_copy(r, direction, 1).wait_recv()
-            r_copy(r, direction, 2).wait_recv()
-        yb[r] = summed(r, 1 - y_hi).astype(BF16)
-        v_copy(r).start()
-
     def write(r):
-        rows = pl.ds(r * 128, 128)
-        mine = summed(r, y_hi) + xres[rows, :].astype(F32)
-        v_copy(r).wait_recv()
-        out_ref[rows, :] = (mine + yr[r].astype(F32)).astype(BF16)
-
-    arrive_q(3)
-
-    @pl.when(has_after)
-    def _():
-        halo_q.start()
-
-    make_gating(3)
-    arrive_q(2)
-    make_gating(2)
-    send_first(3)
-    arrive_q(1)
-    make_gating(1)
-    send_first(2)
-    arrive_q(0)
-
-    @pl.when(has_before)
-    def _():
-        halo_q.wait_recv()
-
-    make_gating(0)
-    send_joined(3)
-    send_first(1)
-    send_joined(2)
-    send_first(0)
-    send_across(3)
-    send_joined(1)
-    send_across(2)
-    write(3)
-    send_joined(0)
-    send_across(1)
-    write(2)
-    send_across(0)
-    write(1)
-    write(0)
+        for index in range(8):
+            place = part_of(index, 1 - core, r)
+            remote(place, place, t_send.at[r, index], t_recv.at[r, index], twin).wait_recv()
+
+        def body(half, carry):
+            rows = pl.ds(r * CHUNK, CHUNK)
+            columns = pl.ds(pl.multiple_of(half * 256, 256), 256)
+            total = xres[rows, columns].astype(F32)
+            for i in range(16):
+                total += jnp.dot(gate[i, rows, :], wo[i, :, columns], preferred_element_type=F32)
+            out_ref[rows, columns] = total.astype(BF16)
+            return carry
+
+        lax.fori_loop(0, 2, body, 0)
+
+    for r in order:
+        arrive_q(r)
+        if r == CHUNKS - 1:
+
+            @pl.when(has_after)
+            def _():
+                halo_q.start()
+
+        if r == 0:
+
+            @pl.when(has_before)
+            def _():
+                halo_q.wait_recv()
+
+        make_gating(r)
+    for r in order:
+        v_arrived(r)
+        a_arrived(0, r)
+    for i in range(15):
+        if i not in SHARED:
+            o_wait(i)
+    for i in SHARED:
+        m_wait(i)
+    for r in order:
+        a_arrived(1, r)
+    for r in order:
+        a_arrived(2, r)
+        write(r)
 
     for direction in range(2):
         for k in range(7):
@@ -525,27 +584,35 @@
         for k in range(3):
             for q in range(PIECES):
                 x_copy(direction, k, q).wait_send()
-    for d in range(2):
-
-        @pl.when(jnp.logical_not(jnp.logical_and(is_home, y_hi == d)))
-        def _():
+    @pl.when(jnp.logical_not(is_home))
+    def _():
+        for d in range(2):
             for q in range(PIECES):
                 y_copy(d, q).wait_send()
+
+    @pl.when(is_home)
+    def _():
+        for q in range(PIECES):
+            f_copy(q).wait_send()
+            f_pass(q).wait_send()
 
     for index in range(8):
         for q in range(PIECES):
             d_copy(index, q, core).wait_send()
     for i in range(2):
         c_kv(i).wait_send()
-    for d in range(8):
-        o_copy(d).wait_send()
-    for r in range(4):
+    for i in range(15):
+        o_copy(i).wait_send()
+    for i in SHARED:
+        m_copy(i).wait_send()
+    for r in range(CHUNKS):
         c_q(r).wait_send()
-        g_copy(r).wait_send()
         v_copy(r).wait_send()
+        for index in range(8):
+            t_copy(index, r).wait_send()
         for direction in range(2):
             for k in range(3):
-                r_copy(r, direction, k).wait_send()
+                a_copy(direction, k, r).wait_send()
 
     @pl.when(has_after)
     def _():
@@ -567,35 +634,34 @@
             pltpu.VMEM((2, 8, ROWS, WIDE), BF16),
             pltpu.VMEM((8, 2, 2, 256, CH), BF16),
             pltpu.VMEM((8, 2, 256, CH), BF16),
+            pltpu.VMEM((ROWS, WIDE), BF16),
             pltpu.VMEM((2, 3, ROWS, CH), F32),
             pltpu.VMEM((3, ROWS, CH), BF16),
             pltpu.VMEM((3, ROWS, CH), BF16),
             pltpu.VMEM((2, ROWS, 128), F32),
             pltpu.VMEM((8, ROWS), F32),
             pltpu.VMEM((8, ROWS), F32),
-            pltpu.VMEM((2, 8, CH, WIDE), BF16),
+            pltpu.VMEM((16, CH, WIDE), BF16),
             pltpu.VMEM((2, 16, TAPS, 2 * TAPS), BF16),
             pltpu.VMEM((3, 16 + ROWS, CH), BF16),
             pltpu.VMEM((128 + ROWS, CH), BF16),
             pltpu.VMEM((ROWS, CH), F32),
-            pltpu.VMEM((2, ROWS, CH), BF16),
-            pltpu.VMEM((4, 2, 3, 128, WIDE), BF16),
-            pltpu.VMEM((4, 2, 3, 128, WIDE), BF16),
-            pltpu.VMEM((4, 128, WIDE), BF16),
-            pltpu.VMEM((4, 128, WIDE), BF16),
+            pltpu.VMEM((16, ROWS, CH), BF16),
             pltpu.VMEM((ROWS, WIDE), BF16),
-            dma((9,)),
+            dma((10,)),
             dma((2, 2, 7)), dma((2, 2, 7)),
             dma((2, PIECES)), dma((2, PIECES)),
+            dma((PIECES,)), dma((PIECES,)),
             dma((2, 3, PIECES)), dma((2, 3, PIECES)),
             dma((8, PIECES)), dma((8, PIECES)),
             dma((6,)), dma((6,)),
             dma, dma,
-            dma((8,)), dma((8,)), dma((8,)),
+            dma((15,)), dma((16,)),
+            dma((12,)), dma((12,)),
             dma((3,)), dma((3,)),
-            dma((4,)), dma((4,)),
-            dma((4, 2, 3)), dma((4, 2, 3)),
-            dma((4,)), dma((4,)),
+            dma((CHUNKS,)), dma((CHUNKS,)),
+            dma((CHUNKS, 2, 3)), dma((CHUNKS, 2, 3)),
+            dma((CHUNKS, 8)), dma((CHUNKS, 8)),
         ],
         compiler_params=pltpu.CompilerParams(
             collective_id=0, has_side_effects=True, vmem_limit_bytes=58 * 1024 * 1024

time: 137 us -> 123 us (0.90)
  the two profiles are of different devices: /device:TPU:1 before, /device:TPU:33 now
where the time goes in v4:
time: 123 us
  Pallas kernels  121 us (98%)
  local copies, waits for them, and re-layouts  1.87 us (2%)
    pallas_call x1, Pallas kernels, block_call(): pl.pallas_call(block_kernel, out_shape=jax.ShapeDtypeStruct((ROWS, WIDE),...  121 us

profile of v4, /device:TPU:33, one launch (start us, length us, event | category | flops | bytes accessed | tf_op | source)
XLA Modules:
  0.0 123.1 jit_solution(1169325219310580164)
XLA Ops:
  0.0 121.2 %block.1 = bf16[512,512]{1,0:T(8,128)(2,1)} custom-call(bf16[512,512]{1,0:T(8,128)(2,1)} %x_hbm.1, f32[16,1,512]{2,1,0:T(1,128)} %bitcast.5, bf16[3,512,256]{2,1,0:T(8,128)(2,1)} %bitcast.4, f32[3,3,256]{2,1,0:T(4,128)} %short_ref.1, f32[16,128]{1,0:T(8,128)} %bitcast.6, f32[1,256]{1,0:T(1,128)} %bitcast.7, bf16[256,8192]{1,0:T(8,128)(2,1)} %wo_hbm.1), custom_call_target="tpu_custom_call" | custom-call | tf_op jit(solution)/shard_map/block/pallas_call | solution.py:627
  121.2 1.9 %copy.9 = bf16[512,512]{1,0:T(8,128)(2,1)} copy(bf16[512,512]{1,0:T(8,128)(2,1)} %block.1) | data formatting | bytes 1048576

commit v5 on v4

--- a/solution.py
+++ b/solution.py
@@ -315,7 +315,30 @@
         x_arrived(1, q)
         taken((2, 3), (q,))
     taken((4, 5), range(PIECES))
+
+    def add_kv(u, low, count, first, chunks):
+        rows = pl.ds(low, count)
+
+        def body(j, carry):
+            f = (x_far * 2 + first + j) % 8
+            lhs0, lhs1 = tg[u, f, rows, 0:256], tg[u, f, rows, 256:512]
+            for p in range(2):
+                part = jnp.dot(lhs0, wkv[f, 0, p], preferred_element_type=F32)
+                part += jnp.dot(lhs1, wkv[f, 1, p], preferred_element_type=F32)
+                acc[u, 1 + p, rows, :] += part
+            return carry
+
+        lax.fori_loop(0, chunks, body, 0)
+
+    for direction in range(2):
+        w_wait(0, direction, 6)
     w_step(1, 2)
+
+    def add_near(i, carry):
+        add_kv(i // 2, pl.multiple_of((i % 2) * 256, 256), 256, 2, 6)
+        return carry
+
+    lax.fori_loop(0, 4, add_near, 0)
     x_arrived(2, 0)
     x_arrived(2, 1)
     taken((6, 7), (0, 1))
@@ -332,19 +355,6 @@
     s_copy = remote(ss, sr, s_send, s_recv, mate)
     s_copy.start()
 
-    def add_kv(u, low, count):
-        rows = pl.ds(low, count)
-
-        def body(f, carry):
-            lhs0, lhs1 = tg[u, f, rows, 0:256], tg[u, f, rows, 256:512]
-            for p in range(2):
-                part = jnp.dot(lhs0, wkv[f, 0, p], preferred_element_type=F32)
-                part += jnp.dot(lhs1, wkv[f, 1, p], preferred_element_type=F32)
-                acc[u, 1 + p, rows, :] += part
-            return carry
-
-        lax.fori_loop(0, 8, body, 0)
-
     def add_q(u, f, low, count):
         rows = pl.ds(low, count)
         part = jnp.dot(tg[u, f, rows, 0:256], wq[f, 0], preferred_element_type=F32)
@@ -368,7 +378,7 @@
         return remote(cs.at[0, rows, :], cr.at[0, rows, :], c_send.at[2 + r], c_recv.at[2 + r], mate)
 
     def give_kv(i):
-        add_kv(other, *kv_cuts[i])
+        add_kv(other, *kv_cuts[i], 0, 2)
         rows = pl.ds(*kv_cuts[i])
         for p in (1, 2):
             cs[p, rows, :] = acc[other, p, rows, :].astype(BF16)
@@ -411,14 +421,12 @@
         product = pe[pl.ds(128 + r * 128, 128), :].astype(F32)
         mix[pl.ds(r * 128, 128), :] = skip_ref[...] * product + mixed
 
-    for direction in range(2):
-        w_wait(0, direction, 6)
     give_kv(0)
     w_step(1, 4)
     give_kv(1)
-    add_kv(y_lo, 240, 272)
+    add_kv(y_lo, 240, 272, 0, 2)
     w_step(1, 5)
-    add_kv(y_lo, 0, 240)
+    add_kv(y_lo, 0, 240, 0, 2)
     w_step(1, 6)
     s_copy.wait()
     total = row_sums(y_lo) + sr[...]
@@ -442,27 +450,10 @@
 
     make_product(2)
     w_step(1, 7)
-    make_mixing(3)
-    for distance in (0, 1, 2):
+    add_q_chunk(z)
+    for distance in (1, 2, 3):
         add_q_chunk((z + distance) % 8)
-        if distance:
-            add_q_chunk((z + 8 - distance) % 8)
-    c_kv(1).wait_recv()
-    for p in (1, 2):
-        finish(p, *kv_cuts[1])
-    make_product(1)
-    make_mixing(2)
-    add_q_chunk((z + 3) % 8)
-    add_q_chunk((z + 5) % 8)
-
-    @pl.when(has_before)
-    def _():
-        for cp in halo_kv:
-            cp.wait_recv()
-
-    make_product(0)
-    make_mixing(1)
-    make_mixing(0)
+        add_q_chunk((z + 8 - distance) % 8)
     o_keep.wait()
     keep_x.wait()
 
@@ -480,6 +471,13 @@
     for low in (256, 0):
         acc[y_lo, 0, pl.ds(low, 256), :] = add_q(y_lo, f_last, low, 256)
 
+    make_mixing(3)
+    c_kv(1).wait_recv()
+    for p in (1, 2):
+        finish(p, *kv_cuts[1])
+    make_product(1)
+    make_mixing(2)
+
     held = [(y_hi, x), (1 - y_hi, x)]
     for y_hi_ in (y_hi, 1 - y_hi):
         held += [(y_hi_, x_left), (y_hi_, x_right)]
@@ -563,6 +561,16 @@
                 halo_q.wait_recv()
 
         make_gating(r)
+        if r == CHUNKS - 1:
+
+            @pl.when(has_before)
+            def _():
+                for cp in halo_kv:
+                    cp.wait_recv()
+
+            make_product(0)
+            make_mixing(1)
+            make_mixing(0)
     for r in order:
         v_arrived(r)
         a_arrived(0, r)

time: 123 us -> 122 us (level)
  the two profiles are of different devices: /device:TPU:33 before, /device:TPU:1 now
where the time goes in v5:
time: 122 us; the launch traced here: 119 us
  Pallas kernels  118 us (97%)
  local copies, waits for them, and re-layouts  1.87 us (2%)
    pallas_call x1, Pallas kernels, block_call(): pl.pallas_call(block_kernel, out_shape=jax.ShapeDtypeStruct((ROWS, WIDE),...  118 us

profile of v5, /device:TPU:1, one launch (start us, length us, event | category | flops | bytes accessed | tf_op | source)
XLA Modules:
  0.0 119.5 jit_solution(9832267842986492437)
XLA Ops:
  0.0 117.6 %block.1 = bf16[512,512]{1,0:T(8,128)(2,1)} custom-call(bf16[512,512]{1,0:T(8,128)(2,1)} %x_hbm.1, f32[16,1,512]{2,1,0:T(1,128)} %bitcast.5, bf16[3,512,256]{2,1,0:T(8,128)(2,1)} %bitcast.4, f32[3,3,256]{2,1,0:T(4,128)} %short_ref.1, f32[16,128]{1,0:T(8,128)} %bitcast.6, f32[1,256]{1,0:T(1,128)} %bitcast.7, bf16[256,8192]{1,0:T(8,128)(2,1)} %wo_hbm.1), custom_call_target="tpu_custom_call" | custom-call | tf_op jit(solution)/shard_map/block/pallas_call | solution.py:635
  117.6 1.9 %copy.9 = bf16[512,512]{1,0:T(8,128)(2,1)} copy(bf16[512,512]{1,0:T(8,128)(2,1)} %block.1) | data formatting | bytes 1048576

commit v6 on v5

--- a/solution.py
+++ b/solution.py
@@ -574,13 +574,13 @@
     for r in order:
         v_arrived(r)
         a_arrived(0, r)
+    for r in order:
+        a_arrived(1, r)
     for i in range(15):
         if i not in SHARED:
             o_wait(i)
     for i in SHARED:
         m_wait(i)
-    for r in order:
-        a_arrived(1, r)
     for r in order:
         a_arrived(2, r)
         write(r)

time: 122 us -> 122 us (level)
  no operation moved by 1% of the time
where the time goes in v6:
time: 122 us; the launch traced here: 119 us
  Pallas kernels  118 us (97%)
  local copies, waits for them, and re-layouts  1.87 us (2%)
    pallas_call x1, Pallas kernels, block_call(): pl.pallas_call(block_kernel, out_shape=jax.ShapeDtypeStruct((ROWS, WIDE),...  118 us

profile of v6, /device:TPU:1, one launch (start us, length us, event | category | flops | bytes accessed | tf_op | source)
XLA Modules:
  0.0 119.5 jit_solution(14186617325296968515)
XLA Ops:
  0.0 117.6 %block.1 = bf16[512,512]{1,0:T(8,128)(2,1)} custom-call(bf16[512,512]{1,0:T(8,128)(2,1)} %x_hbm.1, f32[16,1,512]{2,1,0:T(1,128)} %bitcast.5, bf16[3,512,256]{2,1,0:T(8,128)(2,1)} %bitcast.4, f32[3,3,256]{2,1,0:T(4,128)} %short_ref.1, f32[16,128]{1,0:T(8,128)} %bitcast.6, f32[1,256]{1,0:T(1,128)} %bitcast.7, bf16[256,8192]{1,0:T(8,128)(2,1)} %wo_hbm.1), custom_call_target="tpu_custom_call" | custom-call | tf_op jit(solution)/shard_map/block/pallas_call | solution.py:635
  117.6 1.9 %copy.9 = bf16[512,512]{1,0:T(8,128)(2,1)} copy(bf16[512,512]{1,0:T(8,128)(2,1)} %block.1) | data formatting | bytes 1048576
